TPU v7x, 256 devices: a whole 4x4x8 slice. The times are simulated.
256 devices in a mesh: row: 8 (over x, core), col: 32 (over y, z).
Axes of the slice: x: 4, y: 4, z: 8, core: 2. Of those that a mesh axis runs over, the one named last changes fastest.
Arguments:
- amplitudes: float32 [262144, 1024], P(('row', 'col')), may hold values from -6 to 6
- integrals: float32 [262144, 1024], P(('row', 'col')), may hold values from -0.046875 to 0.046875
- denominators: float32 [1024, 1024], P('col', 'row'), may hold values from 1 to 4
- history: float32 [8, 1024, 1024], P(None, 'col', 'row'), may hold values from -80 to 80
Outputs:
- extrapolated: float32 [1024, 1024], P('col', 'row')
- coefficients: float32 [8], replicated
All inputs are finite; a program needn't handle non-finite values.
Results may differ from a plain program's by a relative error of at most 0.00005.
Values sent between devices are 32-bit elements; how exact they have to be, the bound alone decides.
No kernel may reach another device: no remote copies, remote signals or barrier semaphores. Data moves between devices by JAX's collectives and lax.ppermute only.
A program may use at most 64 MiB of HBM per device.

v0:
```python
import jax
import jax.numpy as jnp
from jax import lax
from jax.experimental import pallas as pl
from jax.experimental.pallas import tpu as pltpu
from jax.sharding import Mesh, PartitionSpec as P

OCC = 32
VBLK = 32
PAIRS = 1024
LANES = 128
HIST = 8
CHUNK = 256
PITCH = 40

SMALL = pltpu.CompilerParams(vmem_limit_bytes=4 * 2**20)


def hot_kernel(hot_ref):
    source = lax.broadcasted_iota(jnp.int32, (PAIRS, LANES), 0)
    lane = lax.broadcasted_iota(jnp.int32, (PAIRS, LANES), 1)
    for g in range(8):
        target = g * LANES + lane
        wanted = (target % VBLK) * VBLK + target // VBLK
        hot_ref[:, g * LANES:(g + 1) * LANES] = jnp.where(source == wanted, 1.0, 0.0).astype(jnp.bfloat16)


def piece_kernel(distance, p_ref, hot_ref, sent_ref, kept_ref, turned):
    chip = lax.rem(lax.axis_index("x") + distance, 4)
    core = lax.axis_index("core")
    wanted = hot_ref[:, pl.ds(pl.multiple_of(chip * 2 * LANES, LANES), 2 * LANES)]
    for k in range(PAIRS // CHUNK):
        p = p_ref[k * CHUNK:(k + 1) * CHUNK, :]
        high = p.astype(jnp.bfloat16)
        low = (p - high.astype(jnp.float32)).astype(jnp.bfloat16)
        flipped = jnp.dot(high, wanted, preferred_element_type=jnp.float32)
        flipped = flipped + jnp.dot(low, wanted, preferred_element_type=jnp.float32)
        for m in range(CHUNK // OCC):
            j = k * (CHUNK // OCC) + m
            for side in range(2):
                turned[side, j * PITCH:j * PITCH + OCC, :] = flipped[m * OCC:(m + 1) * OCC, side * LANES:(side + 1) * LANES]
    for side, out_ref in ((1 - core, sent_ref), (core, kept_ref)):
        columns = pl.ds(pl.multiple_of((chip * 2 + side) * LANES, LANES), LANES)
        for i in range(OCC):
            rows = slice(i * OCC, (i + 1) * OCC)
            out_ref[rows, :] = p_ref[rows, columns] + turned[side, pl.ds(i, OCC, stride=PITCH), :]


def piece(partial, hot, distance):
    def kernel(*refs):
        piece_kernel(distance, *refs)

    out = jax.ShapeDtypeStruct((PAIRS, LANES), jnp.float32)
    return pl.pallas_call(
        kernel,
        out_shape=(out, out),
        scratch_shapes=[pltpu.VMEM((2, OCC * PITCH, LANES), jnp.float32)],
        compiler_params=pltpu.CompilerParams(vmem_limit_bytes=16 * 2**20),
        cost_estimate=pl.CostEstimate(flops=PAIRS**3, bytes_accessed=5 * 2**20, transcendentals=0),
    )(partial, hot)


def join_kernel(kept_ref, came_ref, low_below, high_below, low_above, high_above, joined_ref):
    middle = PAIRS // 2
    for part, (below, above) in enumerate(((low_below, low_above), (high_below, high_above))):
        rows = slice(part * middle, (part + 1) * middle)
        joined_ref[rows, :] = (kept_ref[rows, :] + came_ref[rows, :]) + (below[...] + above[...])


def gram_entry(errors, k, l, lane, message):
    value = jnp.sum(errors[k] * errors[l], keepdims=True)
    return jnp.where(lane == HIST * k + l, value, message)


def prepare_kernel(hist_ref, den_ref, errors_ref, following_ref, den_out_ref, message_ref):
    lane = lax.broadcasted_iota(jnp.int32, (8, LANES), 1)
    errors = [hist_ref[k + 1] - hist_ref[k] for k in range(HIST - 1)]
    message = jnp.zeros((8, LANES), jnp.float32)
    for k in range(HIST - 1):
        errors_ref[k] = errors[k]
        following_ref[k] = hist_ref[k + 1]
        for l in range(k + 1):
            message = gram_entry(errors, k, l, lane, message)
    den_out_ref[...] = den_ref[...]
    message_ref[...] = message


def gram_kernel(parts_ref, den_ref, errors_ref, following_ref, early_ref, update_ref, message_ref):
    total = parts_ref[0]
    for s in range(1, 32):
        total = total + parts_ref[s]
    update = total / den_ref[...]
    update_ref[...] = update
    errors = [errors_ref[k] for k in range(HIST - 1)] + [update - following_ref[HIST - 2]]
    lane = lax.broadcasted_iota(jnp.int32, (8, LANES), 1)
    message = early_ref[...]
    for l in range(HIST):
        message = gram_entry(errors, HIST - 1, l, lane, message)
    for s in range(32):
        message_ref[s * 8:(s + 1) * 8, :] = message


def tail_kernel(grams_ref, update_ref, following_ref, out_ref, coef_ref):
    row = jnp.sum(grams_ref[...], axis=0, keepdims=True)
    spread = (1, LANES)
    a = [[jnp.broadcast_to(row[:, HIST * k + l:HIST * k + l + 1], spread) for l in range(k + 1)] for k in range(HIST)]
    trace = a[0][0]
    for k in range(1, HIST):
        trace = trace + a[k][k]
    ridge = 1e-06 * trace / HIST
    for k in range(HIST):
        a[k][k] = a[k][k] + ridge
    low = [[None] * HIST for _ in range(HIST)]
    inverse = [None] * HIST
    for k in range(HIST):
        pivot = a[k][k]
        for m in range(k):
            pivot = pivot - low[k][m] * low[k][m]
        inverse[k] = 1.0 / jnp.sqrt(pivot)
        for n in range(k + 1, HIST):
            entry = a[n][k]
            for m in range(k):
                entry = entry - low[n][m] * low[k][m]
            low[n][k] = entry * inverse[k]
    half = [None] * HIST
    for k in range(HIST):
        value = jnp.ones(spread, jnp.float32)
        for m in range(k):
            value = value - low[k][m] * half[m]
        half[k] = value * inverse[k]
    whole = [None] * HIST
    for k in reversed(range(HIST)):
        value = half[k]
        for m in range(k + 1, HIST):
            value = value - low[m][k] * whole[m]
        whole[k] = value * inverse[k]
    total = whole[0]
    for k in range(1, HIST):
        total = total + whole[k]
    lane = lax.broadcasted_iota(jnp.int32, spread, 1)
    weights = [whole[k] / total for k in range(HIST)]
    coefficients = jnp.zeros(spread, jnp.float32)
    for k in range(HIST):
        coefficients = jnp.where(lane == k, weights[k], coefficients)
    coef_ref[...] = coefficients[:, :HIST]
    out = weights[HIST - 1] * update_ref[...]
    for k in range(HIST - 1):
        out = out + weights[k] * following_ref[k]
    out_ref[...] = out


def shift(value, axis, distance):
    return lax.ppermute(value, axis, [(i, (i + distance) % 4) for i in range(4)])


def step(amplitudes, integrals, denominators, history):
    block = jax.ShapeDtypeStruct((OCC, LANES), jnp.float32)
    slabs = jax.ShapeDtypeStruct((HIST - 1, OCC, LANES), jnp.float32)
    errors, following, divisors, early = pl.pallas_call(
        prepare_kernel,
        out_shape=(slabs, slabs, block, jax.ShapeDtypeStruct((8, LANES), jnp.float32)),
        cost_estimate=pl.CostEstimate(flops=2**18, bytes_accessed=2**19, transcendentals=0),
        compiler_params=SMALL,
        name="prepare",
    )(history, denominators)
    hot = pl.pallas_call(
        hot_kernel,
        out_shape=jax.ShapeDtypeStruct((PAIRS, PAIRS), jnp.bfloat16),
        compiler_params=SMALL,
        cost_estimate=pl.CostEstimate(flops=2**20, bytes_accessed=2**21, transcendentals=0),
        name="hot",
    )()
    partial = lax.dot_general(
        amplitudes,
        integrals,
        (((0,), (0,)), ((), ())),
        precision=lax.Precision.HIGH,
        preferred_element_type=jnp.float32,
    )
    pieces = {}
    for distance in (2, 1, 3, 0):
        sent, kept = piece(partial, hot, distance)
        came = lax.ppermute(sent, "core", [(0, 1), (1, 0)])
        pieces[distance] = (kept, came)
    middle = PAIRS // 2

    def half(part, whole):
        kept, came = whole
        rows = slice(part * middle, (part + 1) * middle)
        return kept[rows] + came[rows]

    def relayed(part, whole, arrived):
        whole, arrived = lax.optimization_barrier((whole, arrived))
        return half(part, whole) + arrived

    from_below = shift(half(0, pieces[2]), "x", 1)
    from_above = shift(half(1, pieces[2]), "x", 3)
    below = [None, shift(half(1, pieces[1]), "x", 1)]
    above = [shift(half(0, pieces[3]), "x", 3), None]
    below[0] = shift(relayed(0, pieces[1], from_below), "x", 1)
    above[1] = shift(relayed(1, pieces[3], from_above), "x", 3)
    rows = pl.pallas_call(
        join_kernel,
        out_shape=jax.ShapeDtypeStruct((PAIRS, LANES), jnp.float32),
        compiler_params=SMALL,
        name="join",
    )(*pieces[0], *below, *above)
    parts = lax.all_to_all(rows, ("y", "z"), 0, 0, tiled=True).reshape(32, OCC, LANES)
    update, message = pl.pallas_call(
        gram_kernel,
        out_shape=(block, jax.ShapeDtypeStruct((256, LANES), jnp.float32)),
        compiler_params=SMALL,
        name="gram",
    )(parts, divisors, errors, following, early)
    grams = lax.all_to_all(message, ("x", "core", "y", "z"), 0, 0, tiled=True)
    extrapolated, coefficients = pl.pallas_call(
        tail_kernel,
        out_shape=(block, jax.ShapeDtypeStruct((1, HIST), jnp.float32)),
        compiler_params=SMALL,
        name="tail",
    )(grams, update, following)
    return extrapolated, coefficients.reshape(HIST)


def solution(mesh):
    cores = Mesh(mesh.devices.reshape(4, 2, 4, 8), ("x", "core", "y", "z"))
    pairs = P(("x", "core", "y", "z"), None)
    return jax.shard_map(
        step,
        mesh=cores,
        in_specs=(pairs, pairs, P(("y", "z"), ("x", "core")), P(None, ("y", "z"), ("x", "core"))),
        out_specs=(P(("y", "z"), ("x", "core")), P()),
        check_vma=False,
    )
```

profile of v0, /device:TPU:1, one launch (start us, length us, event | category | flops | bytes accessed | tf_op | source)
XLA Modules:
  0.0 92.7 jit_solution(6773141205177305209)
XLA Ops:
  0.6 0.6 hot.1.refs_1_
  1.2 10.1 %fusion.refs_0_ = f32[1024,1024]{1,0:T(8,128)S(1)} fusion(f32[1024,1024]{1,0:T(8,128)} %param.4, f32[1024,1024]{1,0:T(8,128)} %param.5), kind=kOutput, calls=%fused_computation.6 | convolution fusion | flops 6442450944 | bytes 12582912 | tf_op jit(solution)/shard_map/dot_general | solution.py:173
  11.4 1.6 %shard_map.61 = (f32[1024,128]{1,0:T(8,128)S(1)}, f32[1024,128]{1,0:T(8,128)S(1)}) custom-call(f32[1024,1024]{1,0:T(8,128)S(1)} %fusion.refs_0_, bf16[1024,1024]{1,0:T(8,128)(2,1)S(1)} %hot.1.refs_1_), custom_call_target="tpu_custom_call" | custom-call | flops 1073741824 | bytes 5242880 | tf_op jit(solution)/shard_map/pallas_call | solution.py:54
  13.0 3.3 %collective-permute-start.2 = (f32[1024,128]{1,0:T(8,128)S(1)}, f32[1024,128]{1,0:T(8,128)S(1)}, u32[]{:S(2)}, u32[]{:S(2)}) collective-permute-start(f32[1024,128]{1,0:T(8,128)S(1)} %get-tuple-element.29), channel_id=1, source_target_pairs={{0,32},{32,0},{1,33},{33,1},{2,34},{34,2},{3,35},{35,3},{4,36},{36... | collective-permute-start | bytes 1572872 | tf_op jit(solution)/shard_map/ppermute | solution.py:183
  16.3 1.6 %shard_map.62 = (f32[1024,128]{1,0:T(8,128)S(1)}, f32[1024,128]{1,0:T(8,128)S(1)}) custom-call(f32[1024,1024]{1,0:T(8,128)S(1)} %fusion.refs_0_, bf16[1024,1024]{1,0:T(8,128)(2,1)S(1)} %hot.1.refs_1_), custom_call_target="tpu_custom_call" | custom-call | flops 1073741824 | bytes 5242880 | tf_op jit(solution)/shard_map/pallas_call | solution.py:54
  17.8 0.1 collective-permute-start.6
  17.9 1.6 %shard_map.60 = (f32[1024,128]{1,0:T(8,128)S(1)}, f32[1024,128]{1,0:T(8,128)S(1)}) custom-call(f32[1024,1024]{1,0:T(8,128)S(1)} %fusion.refs_0_, bf16[1024,1024]{1,0:T(8,128)(2,1)S(1)} %hot.1.refs_1_), custom_call_target="tpu_custom_call" | custom-call | flops 1073741824 | bytes 5242880 | tf_op jit(solution)/shard_map/pallas_call | solution.py:54
  19.6 0.6 collective-permute-start.1
  20.1 1.6 %shard_map.59 = (f32[1024,128]{1,0:T(8,128)S(1)}, f32[1024,128]{1,0:T(8,128)S(1)}) custom-call(f32[1024,1024]{1,0:T(8,128)S(1)} %fusion.refs_0_, bf16[1024,1024]{1,0:T(8,128)(2,1)S(1)} %hot.1.refs_1_), custom_call_target="tpu_custom_call" | custom-call | flops 1073741824 | bytes 5242880 | tf_op jit(solution)/shard_map/pallas_call | solution.py:54
  21.7 0.1 collective-permute-start
  21.8 0.0 collective-permute-done.2
  21.8 0.0 copy-start
  21.8 0.0 copy-start.1
  21.8 0.1 slice_add_fusion
  21.9 1.1 %collective-permute-start.8 = (f32[512,128]{1,0:T(8,128)S(1)}, f32[512,128]{1,0:T(8,128)S(1)}, u32[]{:S(2)}, u32[]{:S(2)}) collective-permute-start(f32[512,128]{1,0:T(8,128)S(1)} %get-tuple-element.46), channel_id=1, source_target_pairs={{0,192},{64,0},{128,64},{192,128},{1,193},{65,1},{129,65},{193,129... | collective-permute-start | bytes 786440 | tf_op jit(solution)/shard_map/ppermute | solution.py:153
  23.0 0.0 collective-permute-done.6
  23.0 0.6 collective-permute-start.7
  23.6 0.9 %collective-permute-start.3 = (f32[512,128]{1,0:T(8,128)S(1)}, f32[512,128]{1,0:T(8,128)S(1)}, u32[]{:S(2)}, u32[]{:S(2)}) collective-permute-start(f32[512,128]{1,0:T(8,128)S(1)} %get-tuple-element.47), channel_id=1, source_target_pairs={{0,64},{64,128},{128,192},{192,0},{1,65},{65,129},{129,193},{193,1... | collective-permute-start | bytes 786440 | tf_op jit(solution)/shard_map/ppermute | solution.py:153
  24.5 0.0 collective-permute-done.1
  24.6 0.7 collective-permute-start.5
  25.3 4.2 %collective-permute-done.8 = f32[512,128]{1,0:T(8,128)S(1)} collective-permute-done((f32[512,128]{1,0:T(8,128)S(1)}, f32[512,128]{1,0:T(8,128)S(1)}, u32[]{:S(2)}, u32[]{:S(2)}) %collective-permute-start.8) | collective-permute-done | bytes 262176 | tf_op jit(solution)/shard_map/ppermute | solution.py:153
  29.6 0.1 add_add_fusion
  29.6 2.1 %collective-permute-start.9 = (f32[512,128]{1,0:T(8,128)S(1)}, f32[512,128]{1,0:T(8,128)S(1)}, u32[]{:S(2)}, u32[]{:S(2)}) collective-permute-start(f32[512,128]{1,0:T(8,128)S(1)} %add_add_fusion), channel_id=1, source_target_pairs={{0,192},{64,0},{128,64},{192,128},{1,193},{65,1},{129,65},{193,129... | collective-permute-start | bytes 786440 | tf_op jit(solution)/shard_map/ppermute | solution.py:153
  31.7 0.0 collective-permute-done.3
  31.7 0.1 collective-permute-start.4
  31.8 0.0 collective-permute-done.came_ref
  31.8 3.3 %collective-permute-done.7.low_above = f32[512,128]{1,0:T(8,128)S(1)} collective-permute-done((f32[512,128]{1,0:T(8,128)S(1)}, f32[512,128]{1,0:T(8,128)S(1)}, u32[]{:S(2)}, u32[]{:S(2)}) %collective-permute-start.7) | collective-permute-done | bytes 262176 | tf_op jit(solution)/shard_map/ppermute | solution.py:153
  35.2 2.1 %collective-permute-done.5.high_below = f32[512,128]{1,0:T(8,128)S(1)} collective-permute-done((f32[512,128]{1,0:T(8,128)S(1)}, f32[512,128]{1,0:T(8,128)S(1)}, u32[]{:S(2)}, u32[]{:S(2)}) %collective-permute-start.5) | collective-permute-done | bytes 262176 | tf_op jit(solution)/shard_map/ppermute | solution.py:153
  37.3 3.5 %collective-permute-done.9.high_above = f32[512,128]{1,0:T(8,128)S(1)} collective-permute-done((f32[512,128]{1,0:T(8,128)S(1)}, f32[512,128]{1,0:T(8,128)S(1)}, u32[]{:S(2)}, u32[]{:S(2)}) %collective-permute-start.9) | collective-permute-done | bytes 262176 | tf_op jit(solution)/shard_map/ppermute | solution.py:153
  40.8 2.1 %collective-permute-done.4.low_below = f32[512,128]{1,0:T(8,128)S(1)} collective-permute-done((f32[512,128]{1,0:T(8,128)S(1)}, f32[512,128]{1,0:T(8,128)S(1)}, u32[]{:S(2)}, u32[]{:S(2)}) %collective-permute-start.4) | collective-permute-done | bytes 262176 | tf_op jit(solution)/shard_map/ppermute | solution.py:153
  42.9 0.9 %join.1 = f32[1024,128]{1,0:T(8,128)} custom-call(f32[1024,128]{1,0:T(8,128)S(1)} %get-tuple-element.24.kept_ref, f32[1024,128]{1,0:T(8,128)S(1)} %collective-permute-done.came_ref, f32[512,128]{1,0:T(8,128)S(1)} %collective-permute-done.4.low_below, f32[512,128]{1,0:T(8,128)S(1)} %collective-permute-done.5.high_below, ...), custom_call_target="tpu_custom_call" | custom-call | tf_op jit(solution)/shard_map/join/pallas_call | solution.py:202
  43.8 11.2 %all-to-all-start = ((f32[32,32,128]{2,1,0:T(8,128)}), f32[32,32,128]{2,1,0:T(8,128)S(1)}, u32[]{:S(2)}, u32[]{:S(2)}) async-start(f32[32,32,128]{2,1,0:T(8,128)} %bitcast), calls=%async_computation | async-start | bytes 1048576 | tf_op jit(solution)/shard_map/all_to_all | solution.py:208
  55.0 0.0 copy-done
  55.0 0.0 copy-done.1
  55.1 0.2 prepare.1
  55.2 12.8 %all-to-all-done.parts_ref = f32[32,32,128]{2,1,0:T(8,128)S(1)} async-done(((f32[32,32,128]{2,1,0:T(8,128)}), f32[32,32,128]{2,1,0:T(8,128)S(1)}, u32[]{:S(2)}, u32[]{:S(2)}) %all-to-all-start) | async-done | bytes 524320 | tf_op jit(solution)/shard_map/all_to_all | solution.py:208
  68.0 0.2 gram.1
  68.2 23.6 %all_to_all.20 = f32[256,1,128]{2,1,0:T(1,128)S(1)} all-to-all(f32[256,1,128]{2,1,0:T(1,128)S(1)} %bitcast.9), channel_id=1, replica_groups=mesh['x'=4,'core'=2,'y'=4,'z'=8] {'x','core','y','z'}, dimensions={0} | all-to-all | bytes 262144 | tf_op jit(solution)/shard_map/all_to_all | solution.py:215
  91.8 0.9 %tail.1 = (f32[32,128]{1,0:T(8,128)}, f32[1,8]{1,0:T(1,128)}) custom-call(f32[256,128]{1,0:T(8,128)S(1)} %bitcast.8, f32[32,128]{1,0:T(8,128)S(1)} %get-tuple-element.43.update_ref, f32[7,32,128]{2,1,0:T(8,128)S(1)} %get-tuple-element.40.following_ref), custom_call_target="tpu_custom_call" | custom-call | tf_op jit(solution)/shard_map/tail/pallas_call | solution.py:216
  (3 shorter events, 0.1 us)
Async XLA Ops:
  13.0 8.9 %collective-permute-start.2 = (f32[1024,128]{1,0:T(8,128)S(1)}, f32[1024,128]{1,0:T(8,128)S(1)}, u32[]{:S(2)}, u32[]{:S(2)}) collective-permute-start(f32[1024,128]{1,0:T(8,128)S(1)} %get-tuple-element.29), channel_id=1, source_target_pairs={{0,32},{32,0},{1,33},{33,1},{2,34},{34,2},{3,35},{35,3},{4,36},{36... | collective-permute-start | bytes 1572872 | tf_op jit(solution)/shard_map/ppermute | solution.py:183
  17.8 5.1 %collective-permute-start.6 = (f32[1024,128]{1,0:T(8,128)S(1)}, f32[1024,128]{1,0:T(8,128)S(1)}, u32[]{:S(2)}, u32[]{:S(2)}) collective-permute-start(f32[1024,128]{1,0:T(8,128)S(1)} %get-tuple-element.34), channel_id=1, source_target_pairs={{0,32},{32,0},{1,33},{33,1},{2,34},{34,2},{3,35},{35,3},{4,36},{36... | collective-permute-start | bytes 1572872 | tf_op jit(solution)/shard_map/ppermute | solution.py:183
  19.6 5.0 %collective-permute-start.1 = (f32[1024,128]{1,0:T(8,128)S(1)}, f32[1024,128]{1,0:T(8,128)S(1)}, u32[]{:S(2)}, u32[]{:S(2)}) collective-permute-start(f32[1024,128]{1,0:T(8,128)S(1)} %get-tuple-element.27), channel_id=1, source_target_pairs={{0,32},{32,0},{1,33},{33,1},{2,34},{34,2},{3,35},{35,3},{4,36},{36... | collective-permute-start | bytes 1572872 | tf_op jit(solution)/shard_map/ppermute | solution.py:183
  21.7 10.1 %collective-permute-start = (f32[1024,128]{1,0:T(8,128)S(1)}, f32[1024,128]{1,0:T(8,128)S(1)}, u32[]{:S(2)}, u32[]{:S(2)}) collective-permute-start(f32[1024,128]{1,0:T(8,128)S(1)} %get-tuple-element.25), channel_id=1, source_target_pairs={{0,32},{32,0},{1,33},{33,1},{2,34},{34,2},{3,35},{35,3},{4,36},{36... | collective-permute-start | bytes 1572872 | tf_op jit(solution)/shard_map/ppermute | solution.py:183
  21.8 33.2 %copy-start = (f32[8,32,128]{2,1,0:T(8,128)S(1)}, f32[8,32,128]{2,1,0:T(8,128)}, u32[]{:S(2)}) copy-start(f32[8,32,128]{2,1,0:T(8,128)} %hist_ref.1) | copy-start | bytes 393220
  21.8 33.2 %copy-start.1 = (f32[32,128]{1,0:T(8,128)S(1)}, f32[32,128]{1,0:T(8,128)}, u32[]{:S(2)}) copy-start(f32[32,128]{1,0:T(8,128)} %den_ref.1) | copy-start | bytes 49156
  21.9 7.7 %collective-permute-start.8 = (f32[512,128]{1,0:T(8,128)S(1)}, f32[512,128]{1,0:T(8,128)S(1)}, u32[]{:S(2)}, u32[]{:S(2)}) collective-permute-start(f32[512,128]{1,0:T(8,128)S(1)} %get-tuple-element.46), channel_id=1, source_target_pairs={{0,192},{64,0},{128,64},{192,128},{1,193},{65,1},{129,65},{193,129... | collective-permute-start | bytes 786440 | tf_op jit(solution)/shard_map/ppermute | solution.py:153
  23.0 12.2 %collective-permute-start.7 = (f32[512,128]{1,0:T(8,128)S(1)}, f32[512,128]{1,0:T(8,128)S(1)}, u32[]{:S(2)}, u32[]{:S(2)}) collective-permute-start(f32[512,128]{1,0:T(8,128)S(1)} %slice_add_fusion.1), channel_id=1, source_target_pairs={{0,192},{64,0},{128,64},{192,128},{1,193},{65,1},{129,65},{193,129... | collective-permute-start | bytes 786440 | tf_op jit(solution)/shard_map/ppermute | solution.py:153
  23.6 8.1 %collective-permute-start.3 = (f32[512,128]{1,0:T(8,128)S(1)}, f32[512,128]{1,0:T(8,128)S(1)}, u32[]{:S(2)}, u32[]{:S(2)}) collective-permute-start(f32[512,128]{1,0:T(8,128)S(1)} %get-tuple-element.47), channel_id=1, source_target_pairs={{0,64},{64,128},{128,192},{192,0},{1,65},{65,129},{129,193},{193,1... | collective-permute-start | bytes 786440 | tf_op jit(solution)/shard_map/ppermute | solution.py:153
  24.6 12.7 %collective-permute-start.5 = (f32[512,128]{1,0:T(8,128)S(1)}, f32[512,128]{1,0:T(8,128)S(1)}, u32[]{:S(2)}, u32[]{:S(2)}) collective-permute-start(f32[512,128]{1,0:T(8,128)S(1)} %slice_add_fusion.2), channel_id=1, source_target_pairs={{0,64},{64,128},{128,192},{192,0},{1,65},{65,129},{129,193},{193,1... | collective-permute-start | bytes 786440 | tf_op jit(solution)/shard_map/ppermute | solution.py:153
  29.6 11.2 %collective-permute-start.9 = (f32[512,128]{1,0:T(8,128)S(1)}, f32[512,128]{1,0:T(8,128)S(1)}, u32[]{:S(2)}, u32[]{:S(2)}) collective-permute-start(f32[512,128]{1,0:T(8,128)S(1)} %add_add_fusion), channel_id=1, source_target_pairs={{0,192},{64,0},{128,64},{192,128},{1,193},{65,1},{129,65},{193,129... | collective-permute-start | bytes 786440 | tf_op jit(solution)/shard_map/ppermute | solution.py:153
  31.7 11.1 %collective-permute-start.4 = (f32[512,128]{1,0:T(8,128)S(1)}, f32[512,128]{1,0:T(8,128)S(1)}, u32[]{:S(2)}, u32[]{:S(2)}) collective-permute-start(f32[512,128]{1,0:T(8,128)S(1)} %add_add_fusion.1), channel_id=1, source_target_pairs={{0,64},{64,128},{128,192},{192,0},{1,65},{65,129},{129,193},{193,1... | collective-permute-start | bytes 786440 | tf_op jit(solution)/shard_map/ppermute | solution.py:153
  43.8 24.2 %all-to-all-start = ((f32[32,32,128]{2,1,0:T(8,128)}), f32[32,32,128]{2,1,0:T(8,128)S(1)}, u32[]{:S(2)}, u32[]{:S(2)}) async-start(f32[32,32,128]{2,1,0:T(8,128)} %bitcast), calls=%async_computation | async-start | bytes 1048576 | tf_op jit(solution)/shard_map/all_to_all | solution.py:208
where the time goes:
time: 92.9 us; the launch traced here: 92.7 us
  waiting for transfers between devices  28.1 us (30%)
  blocking collectives  23.6 us (25%)
  starting transfers between devices  20.8 us (22%)
  matrix products  10.1 us (11%)
  Pallas kernels  9.14 us (10%)
    all_to_all x1, blocking collectives, step(): grams = lax.all_to_all(message, ('x', 'core', 'y', 'z'), 0, 0, tiled=True)  23.6 us
    ppermute x6, waiting for transfers between devices, shift(): lax.ppermute(value, axis, [(i, (i + distance) % 4) for i in range(4)])  15.3 us
    all_to_all x1, waiting for transfers between devices, step(): lax.all_to_all(rows, ('y', 'z'), 0, 0, tiled=True).reshape(32, OCC, LANES)  12.8 us
    all_to_all x1, starting transfers between devices, step(): lax.all_to_all(rows, ('y', 'z'), 0, 0, tiled=True).reshape(32, OCC, LANES)  11.2 us
    dot_general x1, matrix products, step(): lax.dot_general(amplitudes, integrals, (((0,), (0,)), ((), ())), precisio...  10.1 us
    pallas_call x4, Pallas kernels, piece(): pl.pallas_call(kernel, out_shape=(out, out), scratch_shapes=[pltpu.VMEM((...  6.34 us
    ppermute x6, starting transfers between devices, shift(): lax.ppermute(value, axis, [(i, (i + distance) % 4) for i in range(4)])  5.51 us
    ppermute x4, starting transfers between devices, step(): came = lax.ppermute(sent, 'core', [(0, 1), (1, 0)])  4.09 us
  transfers between devices with their start and end apart: 11, of which 6 were waited for; matrix products, arithmetic and copies ran while one was open for 0% of the time, Pallas kernels for 5%

commit v1 on v0

--- a/solution.py
+++ b/solution.py
@@ -9,6 +9,8 @@
 VBLK = 32
 PAIRS = 1024
 LANES = 128
+LOW = 24
+HIGH = OCC - LOW
 HIST = 8
 CHUNK = 256
 PITCH = 40
@@ -25,46 +27,82 @@
         hot_ref[:, g * LANES:(g + 1) * LANES] = jnp.where(source == wanted, 1.0, 0.0).astype(jnp.bfloat16)
 
 
-def piece_kernel(distance, p_ref, hot_ref, sent_ref, kept_ref, turned):
+def split(p):
+    high = p.astype(jnp.bfloat16)
+    return high, (p - high.astype(jnp.float32)).astype(jnp.bfloat16)
+
+
+def columns(group):
+    return pl.ds(pl.multiple_of(group * LANES, LANES), LANES)
+
+
+def turn(p_ref, wanted, turned, first, count):
+    groups = wanted.shape[1] // LANES
+    for k in range(count // 8):
+        high, low = split(p_ref[first * OCC + k * CHUNK:first * OCC + (k + 1) * CHUNK, :])
+        flipped = jnp.dot(high, wanted, preferred_element_type=jnp.float32)
+        flipped = flipped + jnp.dot(low, wanted, preferred_element_type=jnp.float32)
+        for m in range(8):
+            rows = slice((8 * k + m) * PITCH, (8 * k + m) * PITCH + OCC)
+            for g in range(groups):
+                turned[g, rows, :] = flipped[m * OCC:(m + 1) * OCC, g * LANES:(g + 1) * LANES]
+
+
+def low_kernel(distance, p_ref, hot_ref, sent_ref, kept_ref, turned):
     chip = lax.rem(lax.axis_index("x") + distance, 4)
+    y = lax.axis_index("y")
     core = lax.axis_index("core")
     wanted = hot_ref[:, pl.ds(pl.multiple_of(chip * 2 * LANES, LANES), 2 * LANES)]
-    for k in range(PAIRS // CHUNK):
-        p = p_ref[k * CHUNK:(k + 1) * CHUNK, :]
-        high = p.astype(jnp.bfloat16)
-        low = (p - high.astype(jnp.float32)).astype(jnp.bfloat16)
-        flipped = jnp.dot(high, wanted, preferred_element_type=jnp.float32)
-        flipped = flipped + jnp.dot(low, wanted, preferred_element_type=jnp.float32)
-        for m in range(CHUNK // OCC):
-            j = k * (CHUNK // OCC) + m
-            for side in range(2):
-                turned[side, j * PITCH:j * PITCH + OCC, :] = flipped[m * OCC:(m + 1) * OCC, side * LANES:(side + 1) * LANES]
+    turn(p_ref, wanted, turned, 0, LOW)
     for side, out_ref in ((1 - core, sent_ref), (core, kept_ref)):
-        columns = pl.ds(pl.multiple_of((chip * 2 + side) * LANES, LANES), LANES)
-        for i in range(OCC):
-            rows = slice(i * OCC, (i + 1) * OCC)
-            out_ref[rows, :] = p_ref[rows, columns] + turned[side, pl.ds(i, OCC, stride=PITCH), :]
-
-
-def piece(partial, hot, distance):
-    def kernel(*refs):
-        piece_kernel(distance, *refs)
-
-    out = jax.ShapeDtypeStruct((PAIRS, LANES), jnp.float32)
+        for e in range(4):
+            for z in range(8):
+                i = 8 * lax.rem(y + e, 4) + z
+                straight = p_ref[pl.ds(pl.multiple_of(i * OCC, OCC), LOW), columns(2 * chip + side)]
+                slot = slice((8 * e + z) * LOW, (8 * e + z + 1) * LOW)
+                out_ref[slot, :] = straight + turned[side, pl.ds(i, LOW, stride=PITCH), :]
+
+
+def high_kernel(p_ref, hot_ref, sent_ref, kept_ref, turned):
+    x = lax.axis_index("x")
+    y = lax.axis_index("y")
+    core = lax.axis_index("core")
+    turn(p_ref, hot_ref[...], turned, LOW, HIGH)
+    for e in range(4):
+        for z in range(8):
+            i = 8 * lax.rem(y + e, 4) + z
+            rows = pl.ds(pl.multiple_of(i * OCC + LOW, HIGH), HIGH)
+            for side, out_ref in ((1 - core, sent_ref), (core, kept_ref)):
+                for d in range(4):
+                    g = 2 * lax.rem(x + d, 4) + side
+                    value = p_ref[rows, columns(g)] + turned[g, pl.ds(i, HIGH, stride=PITCH), :]
+                    out_ref[e, d, z * HIGH:(z + 1) * HIGH, :] = value
+
+
+def mirrored(kernel, shape, scratch, partial, hot):
+    out = jax.ShapeDtypeStruct(shape, jnp.float32)
     return pl.pallas_call(
         kernel,
         out_shape=(out, out),
-        scratch_shapes=[pltpu.VMEM((2, OCC * PITCH, LANES), jnp.float32)],
+        scratch_shapes=[pltpu.VMEM(scratch, jnp.float32)],
         compiler_params=pltpu.CompilerParams(vmem_limit_bytes=16 * 2**20),
         cost_estimate=pl.CostEstimate(flops=PAIRS**3, bytes_accessed=5 * 2**20, transcendentals=0),
     )(partial, hot)
 
 
-def join_kernel(kept_ref, came_ref, low_below, high_below, low_above, high_above, joined_ref):
-    middle = PAIRS // 2
-    for part, (below, above) in enumerate(((low_below, low_above), (high_below, high_above))):
-        rows = slice(part * middle, (part + 1) * middle)
-        joined_ref[rows, :] = (kept_ref[rows, :] + came_ref[rows, :]) + (below[...] + above[...])
+def low_piece(partial, hot, distance):
+    def kernel(*refs):
+        low_kernel(distance, *refs)
+
+    return mirrored(kernel, (OCC * LOW, LANES), (2, LOW * PITCH, LANES), partial, hot)
+
+
+def join_kernel(*refs):
+    joined_ref = refs[-1]
+    for part, rows in enumerate((slice(0, LOW), slice(LOW, OCC))):
+        own, a, b, c = refs[4 * part:4 * part + 4]
+        total = (own[...] + a[...]) + (b[...] + c[...])
+        joined_ref[:, rows, :] = total.reshape(8, rows.stop - rows.start, LANES)
 
 
 def gram_entry(errors, k, l, lane, message):
@@ -87,7 +125,7 @@
 
 def gram_kernel(parts_ref, den_ref, errors_ref, following_ref, early_ref, update_ref, message_ref):
     total = parts_ref[0]
-    for s in range(1, 32):
+    for s in range(1, 8):
         total = total + parts_ref[s]
     update = total / den_ref[...]
     update_ref[...] = update
@@ -179,10 +217,10 @@
     )
     pieces = {}
     for distance in (2, 1, 3, 0):
-        sent, kept = piece(partial, hot, distance)
+        sent, kept = low_piece(partial, hot, distance)
         came = lax.ppermute(sent, "core", [(0, 1), (1, 0)])
         pieces[distance] = (kept, came)
-    middle = PAIRS // 2
+    middle = OCC * LOW // 2
 
     def half(part, whole):
         kept, came = whole
@@ -199,13 +237,24 @@
     above = [shift(half(0, pieces[3]), "x", 3), None]
     below[0] = shift(relayed(0, pieces[1], from_below), "x", 1)
     above[1] = shift(relayed(1, pieces[3], from_above), "x", 3)
+    lows = []
+    for h in range(2):
+        lows.append(half(h, pieces[0]) + (below[h] + above[h]))
+    sent, kept = mirrored(high_kernel, (4, 4, 8 * HIGH, LANES), (8, HIGH * PITCH, LANES), partial, hot)
+    came = lax.ppermute(sent, "core", [(0, 1), (1, 0)])
+    high = kept[0] + came[0]
+    for e in (2, 1, 3):
+        high = high + shift(kept[e] + came[e], "y", e)
+    low = [piece for h in range(2) for piece in lows[h].reshape(2, 8 * LOW, LANES)]
+    parts = [low[0]] + [shift(low[e], "y", e) for e in (2, 1, 3)]
+    parts += [high[0]] + [shift(high[d], "x", d) for d in (2, 1, 3)]
     rows = pl.pallas_call(
         join_kernel,
-        out_shape=jax.ShapeDtypeStruct((PAIRS, LANES), jnp.float32),
+        out_shape=jax.ShapeDtypeStruct((8, OCC, LANES), jnp.float32),
         compiler_params=SMALL,
         name="join",
-    )(*pieces[0], *below, *above)
-    parts = lax.all_to_all(rows, ("y", "z"), 0, 0, tiled=True).reshape(32, OCC, LANES)
+    )(*parts)
+    parts = lax.all_to_all(rows, "z", 0, 0, tiled=True)
     update, message = pl.pallas_call(
         gram_kernel,
         out_shape=(block, jax.ShapeDtypeStruct((256, LANES), jnp.float32)),

time: 92.9 us -> 98.6 us (1.061)
  starting transfers between devices: 20.8 us -> 30.9 us
  waiting for transfers between devices: 28.1 us -> 22.8 us
    ppermute x6 -> x15, starting transfers between devices: 5.51 us -> 18 us  [shift(): lax.ppermute(value, axis, [(i, (i + distance) % 4) for i in range(4)])]
    all_to_all x1, waiting for transfers between devices: 12.8 us -> 7.74 us  [step(): parts = lax.all_to_all(rows, 'z', 0, 0, tiled=True)]
    all_to_all x1, starting transfers between devices: 11.2 us -> 8.1 us  [step(): parts = lax.all_to_all(rows, 'z', 0, 0, tiled=True)]
    ppermute x4 -> x5, starting transfers between devices: 4.09 us -> 4.85 us  [step(): came = lax.ppermute(sent, 'core', [(0, 1), (1, 0)])]
    ppermute x6 -> x15, waiting for transfers between devices: 15.3 us -> 15 us  [shift(): lax.ppermute(value, axis, [(i, (i + distance) % 4) for i in range(4)])]
    pallas_call x5 -> x6, Pallas kernels: 7.27 us -> 7.1 us  [the longest x5 6.43 us: mirrored(): pl.pallas_call(kernel, out_shape=(out, out), scratch_shapes=[pltpu.VMEM(s...]
  transfers between devices with their start and end apart: 11 -> 21, of which waited for: 6 -> 7; matrix products, arithmetic and copies ran while one was open for 0% -> 0% of each run, Pallas kernels for 5% -> 5%
where the time goes in v1:
time: 98.6 us; the launch traced here: 98.4 us
  starting transfers between devices  30.9 us (31%)
  blocking collectives  24.4 us (25%)
  waiting for transfers between devices  22.8 us (23%)
  matrix products  10.1 us (10%)
  Pallas kernels  8.95 us (9%)
    all_to_all x1, blocking collectives, step(): grams = lax.all_to_all(message, ('x', 'core', 'y', 'z'), 0, 0, tiled=True)  24.4 us
    ppermute x15, starting transfers between devices, shift(): lax.ppermute(value, axis, [(i, (i + distance) % 4) for i in range(4)])  18 us
    ppermute x15, waiting for transfers between devices, shift(): lax.ppermute(value, axis, [(i, (i + distance) % 4) for i in range(4)])  15 us
    dot_general x1, matrix products, step(): lax.dot_general(amplitudes, integrals, (((0,), (0,)), ((), ())), precisio...  10.1 us
    all_to_all x1, starting transfers between devices, step(): parts = lax.all_to_all(rows, 'z', 0, 0, tiled=True)  8.1 us
    all_to_all x1, waiting for transfers between devices, step(): parts = lax.all_to_all(rows, 'z', 0, 0, tiled=True)  7.74 us
    pallas_call x5, Pallas kernels, mirrored(): pl.pallas_call(kernel, out_shape=(out, out), scratch_shapes=[pltpu.VMEM(s...  6.43 us
    ppermute x5, starting transfers between devices, step(): came = lax.ppermute(sent, 'core', [(0, 1), (1, 0)])  4.85 us
  transfers between devices with their start and end apart: 21, of which 7 were waited for; matrix products, arithmetic and copies ran while one was open for 0% of the time, Pallas kernels for 5%

profile of v1, /device:TPU:1, one launch (start us, length us, event | category | flops | bytes accessed | tf_op | source)
XLA Modules:
  0.0 98.4 jit_solution(8084959681485721924)
XLA Ops:
  0.6 0.6 hot.1.refs_1_.hot_ref
  1.2 10.1 %fusion.11.refs_0_.p_ref = f32[1024,1024]{1,0:T(8,128)S(1)} fusion(f32[1024,1024]{1,0:T(8,128)} %param.4, f32[1024,1024]{1,0:T(8,128)} %param.5), kind=kOutput, calls=%fused_computation.27 | convolution fusion | flops 6442450944 | bytes 12582912 | tf_op jit(solution)/shard_map/dot_general | solution.py:211
  11.4 1.2 %shard_map.61 = (f32[768,128]{1,0:T(8,128)S(1)}, f32[768,128]{1,0:T(8,128)S(1)}) custom-call(f32[1024,1024]{1,0:T(8,128)S(1)} %fusion.11.refs_0_.p_ref, bf16[1024,1024]{1,0:T(8,128)(2,1)S(1)} %hot.1.refs_1_.hot_ref), custom_call_target="tpu_custom_call" | custom-call | flops 1073741824 | bytes 5242880 | tf_op jit(solution)/shard_map/pallas_call | solution.py:84
  12.6 3.3 %collective-permute-start.2 = (f32[768,128]{1,0:T(8,128)S(1)}, f32[768,128]{1,0:T(8,128)S(1)}, u32[]{:S(2)}, u32[]{:S(2)}) collective-permute-start(f32[768,128]{1,0:T(8,128)S(1)} %get-tuple-element.31), channel_id=1, source_target_pairs={{0,32},{32,0},{1,33},{33,1},{2,34},{34,2},{3,35},{35,3},{4,36},{36... | collective-permute-start | bytes 1179656 | tf_op jit(solution)/shard_map/ppermute | solution.py:221
  15.9 1.2 %shard_map.60 = (f32[768,128]{1,0:T(8,128)S(1)}, f32[768,128]{1,0:T(8,128)S(1)}) custom-call(f32[1024,1024]{1,0:T(8,128)S(1)} %fusion.11.refs_0_.p_ref, bf16[1024,1024]{1,0:T(8,128)(2,1)S(1)} %hot.1.refs_1_.hot_ref), custom_call_target="tpu_custom_call" | custom-call | flops 1073741824 | bytes 5242880 | tf_op jit(solution)/shard_map/pallas_call | solution.py:84
  17.1 0.1 collective-permute-start.1
  17.2 1.2 %shard_map.62 = (f32[768,128]{1,0:T(8,128)S(1)}, f32[768,128]{1,0:T(8,128)S(1)}) custom-call(f32[1024,1024]{1,0:T(8,128)S(1)} %fusion.11.refs_0_.p_ref, bf16[1024,1024]{1,0:T(8,128)(2,1)S(1)} %hot.1.refs_1_.hot_ref), custom_call_target="tpu_custom_call" | custom-call | flops 1073741824 | bytes 5242880 | tf_op jit(solution)/shard_map/pallas_call | solution.py:84
  18.4 0.6 collective-permute-start.5
  19.0 1.2 %shard_map.59 = (f32[768,128]{1,0:T(8,128)S(1)}, f32[768,128]{1,0:T(8,128)S(1)}) custom-call(f32[1024,1024]{1,0:T(8,128)S(1)} %fusion.11.refs_0_.p_ref, bf16[1024,1024]{1,0:T(8,128)(2,1)S(1)} %hot.1.refs_1_.hot_ref), custom_call_target="tpu_custom_call" | custom-call | flops 1073741824 | bytes 5242880 | tf_op jit(solution)/shard_map/pallas_call | solution.py:84
  20.2 0.1 collective-permute-start
  20.3 1.6 %shard_map.63 = (f32[4,4,64,128]{3,2,1,0:T(8,128)S(1)}, f32[4,4,64,128]{3,2,1,0:T(8,128)S(1)}) custom-call(f32[1024,1024]{1,0:T(8,128)S(1)} %fusion.11.refs_0_.p_ref, bf16[1024,1024]{1,0:T(8,128)(2,1)S(1)} %hot.1.refs_1_.hot_ref), custom_call_target="tpu_custom_call" | custom-call | flops 1073741824 | bytes 5242880 | tf_op jit(solution)/shard_map/pallas_call | solution.py:84
  21.9 0.8 collective-permute-start.13
  22.7 0.0 collective-permute-done.2
  22.7 0.1 collective-permute-start.3
  22.8 0.0 collective-permute-done.5
  22.8 2.7 %collective-permute-start.8 = (f32[384,128]{1,0:T(8,128)S(1)}, f32[384,128]{1,0:T(8,128)S(1)}, u32[]{:S(2)}, u32[]{:S(2)}) collective-permute-start(f32[384,128]{1,0:T(8,128)S(1)} %get-tuple-element.55), channel_id=1, source_target_pairs={{0,192},{64,0},{128,64},{192,128},{1,193},{65,1},{129,65},{193,129... | collective-permute-start | bytes 589832 | tf_op jit(solution)/shard_map/ppermute | solution.py:191
  25.5 0.0 copy-start
  25.5 0.0 copy-start.1
  25.5 0.0 collective-permute-done.1
  25.5 0.1 collective-permute-start.6
  25.6 0.0 collective-permute-done.13
  25.7 0.1 fusion.4
  25.7 2.5 %collective-permute-start.14 = (f32[4,64,128]{2,1,0:T(8,128)S(1)}, f32[4,64,128]{2,1,0:T(8,128)S(1)}, u32[]{:S(2)}, u32[]{:S(2)}) collective-permute-start(f32[4,64,128]{2,1,0:T(8,128)S(1)} %get-tuple-element.50), channel_id=1, source_target_pairs={{0,16},{8,24},{16,0},{24,8},{1,17},{9,25},{17,1},{25,9},{2,18},{10... | collective-permute-start | bytes 393224 | tf_op jit(solution)/shard_map/ppermute | solution.py:191
  28.3 2.2 %collective-permute-done.3 = f32[384,128]{1,0:T(8,128)S(1)} collective-permute-done((f32[384,128]{1,0:T(8,128)S(1)}, f32[384,128]{1,0:T(8,128)S(1)}, u32[]{:S(2)}, u32[]{:S(2)}) %collective-permute-start.3) | collective-permute-done | bytes 196640 | tf_op jit(solution)/shard_map/ppermute | solution.py:191
  30.4 0.0 collective-permute-start.15
  30.4 0.0 collective-permute-done.8
  30.5 2.7 %collective-permute-start.16 = (f32[4,64,128]{2,1,0:T(8,128)S(1)}, f32[4,64,128]{2,1,0:T(8,128)S(1)}, u32[]{:S(2)}, u32[]{:S(2)}) collective-permute-start(f32[4,64,128]{2,1,0:T(8,128)S(1)} %get-tuple-element.51), channel_id=1, source_target_pairs={{0,24},{8,0},{16,8},{24,16},{1,25},{9,1},{17,9},{25,17},{2,26},{10... | collective-permute-start | bytes 393224 | tf_op jit(solution)/shard_map/ppermute | solution.py:191
  33.2 0.0 collective-permute-done.14
  33.2 0.1 collective-permute-start.7
  33.3 2.5 %collective-permute-done.15 = f32[4,64,128]{2,1,0:T(8,128)S(1)} collective-permute-done((f32[4,64,128]{2,1,0:T(8,128)S(1)}, f32[4,64,128]{2,1,0:T(8,128)S(1)}, u32[]{:S(2)}, u32[]{:S(2)}) %collective-permute-start.15) | collective-permute-done | bytes 131104 | tf_op jit(solution)/shard_map/ppermute | solution.py:191
  35.8 1.0 collective-permute-start.4
  36.8 0.0 collective-permute-done.16
  36.8 1.7 %collective-permute-start.9 = (f32[384,128]{1,0:T(8,128)S(1)}, f32[384,128]{1,0:T(8,128)S(1)}, u32[]{:S(2)}, u32[]{:S(2)}) collective-permute-start(f32[384,128]{1,0:T(8,128)S(1)} %add_add_fusion), channel_id=1, source_target_pairs={{0,192},{64,0},{128,64},{192,128},{1,193},{65,1},{129,65},{193,129... | collective-permute-start | bytes 589832 | tf_op jit(solution)/shard_map/ppermute | solution.py:191
  38.6 0.0 collective-permute-done
  38.6 0.0 collective-permute-done.6
  38.6 0.9 collective-permute-done.7
  39.5 4.4 %collective-permute-done.4 = f32[384,128]{1,0:T(8,128)S(1)} collective-permute-done((f32[384,128]{1,0:T(8,128)S(1)}, f32[384,128]{1,0:T(8,128)S(1)}, u32[]{:S(2)}, u32[]{:S(2)}) %collective-permute-start.4) | collective-permute-done | bytes 196640 | tf_op jit(solution)/shard_map/ppermute | solution.py:191
  44.0 0.0 collective-permute-done.9
  44.0 0.1 fusion
  44.1 1.8 %collective-permute-start.10 = (f32[192,128]{1,0:T(8,128)S(1)}, f32[192,128]{1,0:T(8,128)S(1)}, u32[]{:S(2)}, u32[]{:S(2)}) collective-permute-start(f32[192,128]{1,0:T(8,128)S(1)} %get-tuple-element.58), channel_id=1, source_target_pairs={{0,16},{8,24},{16,0},{24,8},{1,17},{9,25},{17,1},{25,9},{2,18},{10... | collective-permute-start | bytes 294920 | tf_op jit(solution)/shard_map/ppermute | solution.py:191
  45.9 0.1 collective-permute-start.11
  46.0 2.7 %collective-permute-start.12 = (f32[192,128]{1,0:T(8,128)S(1)}, f32[192,128]{1,0:T(8,128)S(1)}, u32[]{:S(2)}, u32[]{:S(2)}) collective-permute-start(f32[192,128]{1,0:T(8,128)S(1)} %get-tuple-element.57), channel_id=1, source_target_pairs={{0,24},{8,0},{16,8},{24,16},{1,25},{9,1},{17,9},{25,17},{2,26},{10... | collective-permute-start | bytes 294920 | tf_op jit(solution)/shard_map/ppermute | solution.py:191
  48.7 0.1 collective-permute-start.17
  48.8 1.6 %collective-permute-start.18 = (f32[64,128]{1,0:T(8,128)S(1)}, f32[64,128]{1,0:T(8,128)S(1)}, u32[]{:S(2)}, u32[]{:S(2)}) collective-permute-start(f32[64,128]{1,0:T(8,128)S(1)} %get-tuple-element.62), channel_id=1, source_target_pairs={{0,64},{64,128},{128,192},{192,0},{1,65},{65,129},{129,193},{193,1... | collective-permute-start | bytes 98312 | tf_op jit(solution)/shard_map/ppermute | solution.py:191
  50.4 2.8 %collective-permute-done.17.refs_5_ = f32[64,128]{1,0:T(8,128)S(1)} collective-permute-done((f32[64,128]{1,0:T(8,128)S(1)}, f32[64,128]{1,0:T(8,128)S(1)}, u32[]{:S(2)}, u32[]{:S(2)}) %collective-permute-start.17) | collective-permute-done | bytes 32800 | tf_op jit(solution)/shard_map/ppermute | solution.py:191
  53.1 0.9 collective-permute-start.19
  54.1 0.0 collective-permute-done.18.refs_6_
  54.1 2.1 %collective-permute-done.19.refs_7_ = f32[64,128]{1,0:T(8,128)S(1)} collective-permute-done((f32[64,128]{1,0:T(8,128)S(1)}, f32[64,128]{1,0:T(8,128)S(1)}, u32[]{:S(2)}, u32[]{:S(2)}) %collective-permute-start.19) | collective-permute-done | bytes 32800 | tf_op jit(solution)/shard_map/ppermute | solution.py:191
  56.2 0.0 collective-permute-done.10.refs_1_
  56.2 0.0 collective-permute-done.11.refs_2_
  56.2 0.0 collective-permute-done.12.refs_3_
  56.2 0.7 join.1
  56.9 8.1 %all-to-all-start = ((f32[8,32,128]{2,1,0:T(8,128)}), f32[8,32,128]{2,1,0:T(8,128)S(1)}, u32[]{:S(2)}, u32[]{:S(2)}) async-start(f32[8,32,128]{2,1,0:T(8,128)} %join.1), calls=%async_computation | async-start | bytes 262144 | tf_op jit(solution)/shard_map/all_to_all | solution.py:257
  65.0 0.0 copy-done
  65.0 0.0 copy-done.1
  65.0 0.2 prepare.1
  65.2 7.7 %all-to-all-done.parts_ref = f32[8,32,128]{2,1,0:T(8,128)S(1)} async-done(((f32[8,32,128]{2,1,0:T(8,128)}), f32[8,32,128]{2,1,0:T(8,128)S(1)}, u32[]{:S(2)}, u32[]{:S(2)}) %all-to-all-start) | async-done | bytes 131104 | tf_op jit(solution)/shard_map/all_to_all | solution.py:257
  72.9 0.1 gram.1
  73.1 24.4 %all_to_all.16 = f32[256,1,128]{2,1,0:T(1,128)S(1)} all-to-all(f32[256,1,128]{2,1,0:T(1,128)S(1)} %bitcast.30), channel_id=1, replica_groups=mesh['x'=4,'core'=2,'y'=4,'z'=8] {'x','core','y','z'}, dimensions={0} | all-to-all | bytes 262144 | tf_op jit(solution)/shard_map/all_to_all | solution.py:264
  97.5 0.9 tail.1
  (9 shorter events, 0.2 us)
Async XLA Ops:
  12.6 10.1 %collective-permute-start.2 = (f32[768,128]{1,0:T(8,128)S(1)}, f32[768,128]{1,0:T(8,128)S(1)}, u32[]{:S(2)}, u32[]{:S(2)}) collective-permute-start(f32[768,128]{1,0:T(8,128)S(1)} %get-tuple-element.31), channel_id=1, source_target_pairs={{0,32},{32,0},{1,33},{33,1},{2,34},{34,2},{3,35},{35,3},{4,36},{36... | collective-permute-start | bytes 1179656 | tf_op jit(solution)/shard_map/ppermute | solution.py:221
  17.1 8.4 %collective-permute-start.1 = (f32[768,128]{1,0:T(8,128)S(1)}, f32[768,128]{1,0:T(8,128)S(1)}, u32[]{:S(2)}, u32[]{:S(2)}) collective-permute-start(f32[768,128]{1,0:T(8,128)S(1)} %get-tuple-element.29), channel_id=1, source_target_pairs={{0,32},{32,0},{1,33},{33,1},{2,34},{34,2},{3,35},{35,3},{4,36},{36... | collective-permute-start | bytes 1179656 | tf_op jit(solution)/shard_map/ppermute | solution.py:221
  18.4 4.4 %collective-permute-start.5 = (f32[768,128]{1,0:T(8,128)S(1)}, f32[768,128]{1,0:T(8,128)S(1)}, u32[]{:S(2)}, u32[]{:S(2)}) collective-permute-start(f32[768,128]{1,0:T(8,128)S(1)} %get-tuple-element.36), channel_id=1, source_target_pairs={{0,32},{32,0},{1,33},{33,1},{2,34},{34,2},{3,35},{35,3},{4,36},{36... | collective-permute-start | bytes 1179656 | tf_op jit(solution)/shard_map/ppermute | solution.py:221
  20.2 18.3 %collective-permute-start = (f32[768,128]{1,0:T(8,128)S(1)}, f32[768,128]{1,0:T(8,128)S(1)}, u32[]{:S(2)}, u32[]{:S(2)}) collective-permute-start(f32[768,128]{1,0:T(8,128)S(1)} %get-tuple-element.27), channel_id=1, source_target_pairs={{0,32},{32,0},{1,33},{33,1},{2,34},{34,2},{3,35},{35,3},{4,36},{36... | collective-permute-start | bytes 1179656 | tf_op jit(solution)/shard_map/ppermute | solution.py:221
  21.9 3.7 %collective-permute-start.13 = (f32[4,4,64,128]{3,2,1,0:T(8,128)S(1)}, f32[4,4,64,128]{3,2,1,0:T(8,128)S(1)}, u32[]{:S(2)}, u32[]{:S(2)}) collective-permute-start(f32[4,4,64,128]{3,2,1,0:T(8,128)S(1)} %get-tuple-element.41), channel_id=1, source_target_pairs={{0,32},{32,0},{1,33},{33,1},{2,34},{34,2},{3,35},{35,3},{4,36},{36... | collective-permute-start | bytes 1572872 | tf_op jit(solution)/shard_map/ppermute | solution.py:244
  22.7 7.7 %collective-permute-start.3 = (f32[384,128]{1,0:T(8,128)S(1)}, f32[384,128]{1,0:T(8,128)S(1)}, u32[]{:S(2)}, u32[]{:S(2)}) collective-permute-start(f32[384,128]{1,0:T(8,128)S(1)} %get-tuple-element.56), channel_id=1, source_target_pairs={{0,64},{64,128},{128,192},{192,0},{1,65},{65,129},{129,193},{193,1... | collective-permute-start | bytes 589832 | tf_op jit(solution)/shard_map/ppermute | solution.py:191
  22.8 7.6 %collective-permute-start.8 = (f32[384,128]{1,0:T(8,128)S(1)}, f32[384,128]{1,0:T(8,128)S(1)}, u32[]{:S(2)}, u32[]{:S(2)}) collective-permute-start(f32[384,128]{1,0:T(8,128)S(1)} %get-tuple-element.55), channel_id=1, source_target_pairs={{0,192},{64,0},{128,64},{192,128},{1,193},{65,1},{129,65},{193,129... | collective-permute-start | bytes 589832 | tf_op jit(solution)/shard_map/ppermute | solution.py:191
  25.5 39.5 %copy-start = (f32[8,32,128]{2,1,0:T(8,128)S(1)}, f32[8,32,128]{2,1,0:T(8,128)}, u32[]{:S(2)}) copy-start(f32[8,32,128]{2,1,0:T(8,128)} %hist_ref.1) | copy-start | bytes 393220
  25.5 39.5 %copy-start.1 = (f32[32,128]{1,0:T(8,128)S(1)}, f32[32,128]{1,0:T(8,128)}, u32[]{:S(2)}) copy-start(f32[32,128]{1,0:T(8,128)} %den_ref.1) | copy-start | bytes 49156
  25.5 13.0 %collective-permute-start.6 = (f32[384,128]{1,0:T(8,128)S(1)}, f32[384,128]{1,0:T(8,128)S(1)}, u32[]{:S(2)}, u32[]{:S(2)}) collective-permute-start(f32[384,128]{1,0:T(8,128)S(1)} %slice_add_fusion.3), channel_id=1, source_target_pairs={{0,192},{64,0},{128,64},{192,128},{1,193},{65,1},{129,65},{193,129... | collective-permute-start | bytes 589832 | tf_op jit(solution)/shard_map/ppermute | solution.py:191
  25.7 7.5 %collective-permute-start.14 = (f32[4,64,128]{2,1,0:T(8,128)S(1)}, f32[4,64,128]{2,1,0:T(8,128)S(1)}, u32[]{:S(2)}, u32[]{:S(2)}) collective-permute-start(f32[4,64,128]{2,1,0:T(8,128)S(1)} %get-tuple-element.50), channel_id=1, source_target_pairs={{0,16},{8,24},{16,0},{24,8},{1,17},{9,25},{17,1},{25,9},{2,18},{10... | collective-permute-start | bytes 393224 | tf_op jit(solution)/shard_map/ppermute | solution.py:191
  30.4 5.4 %collective-permute-start.15 = (f32[4,64,128]{2,1,0:T(8,128)S(1)}, f32[4,64,128]{2,1,0:T(8,128)S(1)}, u32[]{:S(2)}, u32[]{:S(2)}) collective-permute-start(f32[4,64,128]{2,1,0:T(8,128)S(1)} %get-tuple-element.52), channel_id=1, source_target_pairs={{0,8},{8,16},{16,24},{24,0},{1,9},{9,17},{17,25},{25,1},{2,10},{10... | collective-permute-start | bytes 393224 | tf_op jit(solution)/shard_map/ppermute | solution.py:191
  30.5 6.3 %collective-permute-start.16 = (f32[4,64,128]{2,1,0:T(8,128)S(1)}, f32[4,64,128]{2,1,0:T(8,128)S(1)}, u32[]{:S(2)}, u32[]{:S(2)}) collective-permute-start(f32[4,64,128]{2,1,0:T(8,128)S(1)} %get-tuple-element.51), channel_id=1, source_target_pairs={{0,24},{8,0},{16,8},{24,16},{1,25},{9,1},{17,9},{25,17},{2,26},{10... | collective-permute-start | bytes 393224 | tf_op jit(solution)/shard_map/ppermute | solution.py:191
  33.2 6.3 %collective-permute-start.7 = (f32[384,128]{1,0:T(8,128)S(1)}, f32[384,128]{1,0:T(8,128)S(1)}, u32[]{:S(2)}, u32[]{:S(2)}) collective-permute-start(f32[384,128]{1,0:T(8,128)S(1)} %slice_add_fusion.1), channel_id=1, source_target_pairs={{0,64},{64,128},{128,192},{192,0},{1,65},{65,129},{129,193},{193,1... | collective-permute-start | bytes 589832 | tf_op jit(solution)/shard_map/ppermute | solution.py:191
  35.8 8.1 %collective-permute-start.4 = (f32[384,128]{1,0:T(8,128)S(1)}, f32[384,128]{1,0:T(8,128)S(1)}, u32[]{:S(2)}, u32[]{:S(2)}) collective-permute-start(f32[384,128]{1,0:T(8,128)S(1)} %add_add_fusion.1), channel_id=1, source_target_pairs={{0,64},{64,128},{128,192},{192,0},{1,65},{65,129},{129,193},{193,1... | collective-permute-start | bytes 589832 | tf_op jit(solution)/shard_map/ppermute | solution.py:191
  36.8 7.2 %collective-permute-start.9 = (f32[384,128]{1,0:T(8,128)S(1)}, f32[384,128]{1,0:T(8,128)S(1)}, u32[]{:S(2)}, u32[]{:S(2)}) collective-permute-start(f32[384,128]{1,0:T(8,128)S(1)} %add_add_fusion), channel_id=1, source_target_pairs={{0,192},{64,0},{128,64},{192,128},{1,193},{65,1},{129,65},{193,129... | collective-permute-start | bytes 589832 | tf_op jit(solution)/shard_map/ppermute | solution.py:191
  44.1 12.1 %collective-permute-start.10 = (f32[192,128]{1,0:T(8,128)S(1)}, f32[192,128]{1,0:T(8,128)S(1)}, u32[]{:S(2)}, u32[]{:S(2)}) collective-permute-start(f32[192,128]{1,0:T(8,128)S(1)} %get-tuple-element.58), channel_id=1, source_target_pairs={{0,16},{8,24},{16,0},{24,8},{1,17},{9,25},{17,1},{25,9},{2,18},{10... | collective-permute-start | bytes 294920 | tf_op jit(solution)/shard_map/ppermute | solution.py:191
  45.9 10.3 %collective-permute-start.11 = (f32[192,128]{1,0:T(8,128)S(1)}, f32[192,128]{1,0:T(8,128)S(1)}, u32[]{:S(2)}, u32[]{:S(2)}) collective-permute-start(f32[192,128]{1,0:T(8,128)S(1)} %get-tuple-element.59), channel_id=1, source_target_pairs={{0,8},{8,16},{16,24},{24,0},{1,9},{9,17},{17,25},{25,1},{2,10},{10... | collective-permute-start | bytes 294920 | tf_op jit(solution)/shard_map/ppermute | solution.py:191
  46.0 10.2 %collective-permute-start.12 = (f32[192,128]{1,0:T(8,128)S(1)}, f32[192,128]{1,0:T(8,128)S(1)}, u32[]{:S(2)}, u32[]{:S(2)}) collective-permute-start(f32[192,128]{1,0:T(8,128)S(1)} %get-tuple-element.57), channel_id=1, source_target_pairs={{0,24},{8,0},{16,8},{24,16},{1,25},{9,1},{17,9},{25,17},{2,26},{10... | collective-permute-start | bytes 294920 | tf_op jit(solution)/shard_map/ppermute | solution.py:191
  48.7 4.5 %collective-permute-start.17 = (f32[64,128]{1,0:T(8,128)S(1)}, f32[64,128]{1,0:T(8,128)S(1)}, u32[]{:S(2)}, u32[]{:S(2)}) collective-permute-start(f32[64,128]{1,0:T(8,128)S(1)} %get-tuple-element.63), channel_id=1, source_target_pairs={{0,128},{64,192},{128,0},{192,64},{1,129},{65,193},{129,1},{193,65... | collective-permute-start | bytes 98312 | tf_op jit(solution)/shard_map/ppermute | solution.py:191
  48.8 5.3 %collective-permute-start.18 = (f32[64,128]{1,0:T(8,128)S(1)}, f32[64,128]{1,0:T(8,128)S(1)}, u32[]{:S(2)}, u32[]{:S(2)}) collective-permute-start(f32[64,128]{1,0:T(8,128)S(1)} %get-tuple-element.62), channel_id=1, source_target_pairs={{0,64},{64,128},{128,192},{192,0},{1,65},{65,129},{129,193},{193,1... | collective-permute-start | bytes 98312 | tf_op jit(solution)/shard_map/ppermute | solution.py:191
  53.1 3.1 %collective-permute-start.19 = (f32[64,128]{1,0:T(8,128)S(1)}, f32[64,128]{1,0:T(8,128)S(1)}, u32[]{:S(2)}, u32[]{:S(2)}) collective-permute-start(f32[64,128]{1,0:T(8,128)S(1)} %get-tuple-element.61), channel_id=1, source_target_pairs={{0,192},{64,0},{128,64},{192,128},{1,193},{65,1},{129,65},{193,129... | collective-permute-start | bytes 98312 | tf_op jit(solution)/shard_map/ppermute | solution.py:191
  56.9 16.0 %all-to-all-start = ((f32[8,32,128]{2,1,0:T(8,128)}), f32[8,32,128]{2,1,0:T(8,128)S(1)}, u32[]{:S(2)}, u32[]{:S(2)}) async-start(f32[8,32,128]{2,1,0:T(8,128)} %join.1), calls=%async_computation | async-start | bytes 262144 | tf_op jit(solution)/shard_map/all_to_all | solution.py:257

commit v2 on v1

--- a/solution.py
+++ b/solution.py
@@ -220,34 +220,22 @@
         sent, kept = low_piece(partial, hot, distance)
         came = lax.ppermute(sent, "core", [(0, 1), (1, 0)])
         pieces[distance] = (kept, came)
-    middle = OCC * LOW // 2
-
-    def half(part, whole):
-        kept, came = whole
-        rows = slice(part * middle, (part + 1) * middle)
-        return kept[rows] + came[rows]
-
-    def relayed(part, whole, arrived):
-        whole, arrived = lax.optimization_barrier((whole, arrived))
-        return half(part, whole) + arrived
-
-    from_below = shift(half(0, pieces[2]), "x", 1)
-    from_above = shift(half(1, pieces[2]), "x", 3)
-    below = [None, shift(half(1, pieces[1]), "x", 1)]
-    above = [shift(half(0, pieces[3]), "x", 3), None]
-    below[0] = shift(relayed(0, pieces[1], from_below), "x", 1)
-    above[1] = shift(relayed(1, pieces[3], from_above), "x", 3)
-    lows = []
-    for h in range(2):
-        lows.append(half(h, pieces[0]) + (below[h] + above[h]))
+    low = pieces[0][0] + pieces[0][1]
+    for d in (2, 1, 3):
+        low = low + shift(pieces[d][0] + pieces[d][1], "x", d)
+    low = low.reshape(4, 8 * LOW, LANES)
     sent, kept = mirrored(high_kernel, (4, 4, 8 * HIGH, LANES), (8, HIGH * PITCH, LANES), partial, hot)
     came = lax.ppermute(sent, "core", [(0, 1), (1, 0)])
     high = kept[0] + came[0]
     for e in (2, 1, 3):
         high = high + shift(kept[e] + came[e], "y", e)
-    low = [piece for h in range(2) for piece in lows[h].reshape(2, 8 * LOW, LANES)]
-    parts = [low[0]] + [shift(low[e], "y", e) for e in (2, 1, 3)]
-    parts += [high[0]] + [shift(high[d], "x", d) for d in (2, 1, 3)]
+    quarters = [high[0]]
+    for d in (2, 1, 3):
+        quarters.append(shift(high[d], "x", d))
+    parts = [low[0]]
+    for e in (2, 1, 3):
+        parts.append(shift(low[e], "y", e))
+    parts += quarters
     rows = pl.pallas_call(
         join_kernel,
         out_shape=jax.ShapeDtypeStruct((8, OCC, LANES), jnp.float32),

time: 98.6 us -> 99.4 us (level)
  starting transfers between devices: 30.9 us -> 32.9 us
  blocking collectives: 24.4 us -> 23 us
    ppermute x15 -> x12, starting transfers between devices: 18 us -> 19.5 us  [shift(): lax.ppermute(value, axis, [(i, (i + distance) % 4) for i in range(4)])]
    all_to_all x1, blocking collectives: 24.4 us -> 23 us  [step(): grams = lax.all_to_all(message, ('x', 'core', 'y', 'z'), 0, 0, tiled=True)]
    ppermute x15 -> x12, waiting for transfers between devices: 15 us -> 15.3 us  [shift(): lax.ppermute(value, axis, [(i, (i + distance) % 4) for i in range(4)])]
  transfers between devices with their start and end apart: 21 -> 18, of which waited for: 7 -> 6; matrix products, arithmetic and copies ran while one was open for 0% -> 0% of each run, Pallas kernels for 5% -> 5%
where the time goes in v2:
time: 99.4 us; the launch traced here: 99.2 us
  starting transfers between devices  32.9 us (33%)
  waiting for transfers between devices  23 us (23%)
  blocking collectives  23 us (23%)
  matrix products  10.1 us (10%)
  Pallas kernels  8.93 us (9%)
    all_to_all x1, blocking collectives, step(): grams = lax.all_to_all(message, ('x', 'core', 'y', 'z'), 0, 0, tiled=True)  23 us
    ppermute x12, starting transfers between devices, shift(): lax.ppermute(value, axis, [(i, (i + distance) % 4) for i in range(4)])  19.5 us
    ppermute x12, waiting for transfers between devices, shift(): lax.ppermute(value, axis, [(i, (i + distance) % 4) for i in range(4)])  15.3 us
    dot_general x1, matrix products, step(): lax.dot_general(amplitudes, integrals, (((0,), (0,)), ((), ())), precisio...  10.1 us
    all_to_all x1, starting transfers between devices, step(): parts = lax.all_to_all(rows, 'z', 0, 0, tiled=True)  8.16 us
    all_to_all x1, waiting for transfers between devices, step(): parts = lax.all_to_all(rows, 'z', 0, 0, tiled=True)  7.74 us
    pallas_call x5, Pallas kernels, mirrored(): pl.pallas_call(kernel, out_shape=(out, out), scratch_shapes=[pltpu.VMEM(s...  6.4 us
    ppermute x5, starting transfers between devices, step(): came = lax.ppermute(sent, 'core', [(0, 1), (1, 0)])  5.23 us
  transfers between devices with their start and end apart: 18, of which 6 were waited for; matrix products, arithmetic and copies ran while one was open for 0% of the time, Pallas kernels for 5%

profile of v2, /device:TPU:1, one launch (start us, length us, event | category | flops | bytes accessed | tf_op | source)
XLA Modules:
  0.0 99.2 jit_solution(7539451354605527568)
XLA Ops:
  0.6 0.6 hot.1.refs_1_.hot_ref
  1.2 10.1 %fusion.8.refs_0_.p_ref = f32[1024,1024]{1,0:T(8,128)S(1)} fusion(f32[1024,1024]{1,0:T(8,128)} %param.4, f32[1024,1024]{1,0:T(8,128)} %param.5), kind=kOutput, calls=%fused_computation.17 | convolution fusion | flops 6442450944 | bytes 12582912 | tf_op jit(solution)/shard_map/dot_general | solution.py:211
  11.4 1.6 %shard_map.63 = (f32[4,4,64,128]{3,2,1,0:T(8,128)S(1)}, f32[4,4,64,128]{3,2,1,0:T(8,128)S(1)}) custom-call(f32[1024,1024]{1,0:T(8,128)S(1)} %fusion.8.refs_0_.p_ref, bf16[1024,1024]{1,0:T(8,128)(2,1)S(1)} %hot.1.refs_1_.hot_ref), custom_call_target="tpu_custom_call" | custom-call | flops 1073741824 | bytes 5242880 | tf_op jit(solution)/shard_map/pallas_call | solution.py:84
  13.0 3.3 %collective-permute-start.10 = (f32[4,4,64,128]{3,2,1,0:T(8,128)S(1)}, f32[4,4,64,128]{3,2,1,0:T(8,128)S(1)}, u32[]{:S(2)}, u32[]{:S(2)}) collective-permute-start(f32[4,4,64,128]{3,2,1,0:T(8,128)S(1)} %get-tuple-element.29), channel_id=1, source_target_pairs={{0,32},{32,0},{1,33},{33,1},{2,34},{34,2},{3,35},{35,3},{4,36},{36... | collective-permute-start | bytes 1572872 | tf_op jit(solution)/shard_map/ppermute | solution.py:228
  16.2 1.2 %shard_map.60 = (f32[768,128]{1,0:T(8,128)S(1)}, f32[768,128]{1,0:T(8,128)S(1)}) custom-call(f32[1024,1024]{1,0:T(8,128)S(1)} %fusion.8.refs_0_.p_ref, bf16[1024,1024]{1,0:T(8,128)(2,1)S(1)} %hot.1.refs_1_.hot_ref), custom_call_target="tpu_custom_call" | custom-call | flops 1073741824 | bytes 5242880 | tf_op jit(solution)/shard_map/pallas_call | solution.py:84
  17.5 0.1 collective-permute-start.1
  17.6 1.2 %shard_map.61 = (f32[768,128]{1,0:T(8,128)S(1)}, f32[768,128]{1,0:T(8,128)S(1)}) custom-call(f32[1024,1024]{1,0:T(8,128)S(1)} %fusion.8.refs_0_.p_ref, bf16[1024,1024]{1,0:T(8,128)(2,1)S(1)} %hot.1.refs_1_.hot_ref), custom_call_target="tpu_custom_call" | custom-call | flops 1073741824 | bytes 5242880 | tf_op jit(solution)/shard_map/pallas_call | solution.py:84
  18.8 0.6 collective-permute-start.3
  19.4 1.2 %shard_map.62 = (f32[768,128]{1,0:T(8,128)S(1)}, f32[768,128]{1,0:T(8,128)S(1)}) custom-call(f32[1024,1024]{1,0:T(8,128)S(1)} %fusion.8.refs_0_.p_ref, bf16[1024,1024]{1,0:T(8,128)(2,1)S(1)} %hot.1.refs_1_.hot_ref), custom_call_target="tpu_custom_call" | custom-call | flops 1073741824 | bytes 5242880 | tf_op jit(solution)/shard_map/pallas_call | solution.py:84
  20.6 0.1 collective-permute-start.5
  20.7 0.0 collective-permute-done.10
  20.7 1.3 %collective-permute-start.11 = (f32[4,64,128]{2,1,0:T(8,128)S(1)}, f32[4,64,128]{2,1,0:T(8,128)S(1)}, u32[]{:S(2)}, u32[]{:S(2)}) collective-permute-start(f32[4,64,128]{2,1,0:T(8,128)S(1)} %get-tuple-element.38), channel_id=1, source_target_pairs={{0,16},{8,24},{16,0},{24,8},{1,17},{9,25},{17,1},{25,9},{2,18},{10... | collective-permute-start | bytes 393224 | tf_op jit(solution)/shard_map/ppermute | solution.py:191
  22.1 0.4 collective-permute-start.12
  22.5 1.2 %shard_map.59 = (f32[768,128]{1,0:T(8,128)S(1)}, f32[768,128]{1,0:T(8,128)S(1)}) custom-call(f32[1024,1024]{1,0:T(8,128)S(1)} %fusion.8.refs_0_.p_ref, bf16[1024,1024]{1,0:T(8,128)(2,1)S(1)} %hot.1.refs_1_.hot_ref), custom_call_target="tpu_custom_call" | custom-call | flops 1073741824 | bytes 5242880 | tf_op jit(solution)/shard_map/pallas_call | solution.py:84
  23.7 0.0 collective-permute-done.1
  23.7 1.1 %collective-permute-start = (f32[768,128]{1,0:T(8,128)S(1)}, f32[768,128]{1,0:T(8,128)S(1)}, u32[]{:S(2)}, u32[]{:S(2)}) collective-permute-start(f32[768,128]{1,0:T(8,128)S(1)} %get-tuple-element.21), channel_id=1, source_target_pairs={{0,32},{32,0},{1,33},{33,1},{2,34},{34,2},{3,35},{35,3},{4,36},{36... | collective-permute-start | bytes 1179656 | tf_op jit(solution)/shard_map/ppermute | solution.py:221
  24.8 0.0 copy-start
  24.8 0.0 copy-start.1
  24.9 0.0 collective-permute-done.3
  24.9 2.8 %collective-permute-start.2 = (f32[768,128]{1,0:T(8,128)S(1)}, f32[768,128]{1,0:T(8,128)S(1)}, u32[]{:S(2)}, u32[]{:S(2)}) collective-permute-start(f32[768,128]{1,0:T(8,128)S(1)} %add.55), channel_id=1, source_target_pairs={{0,128},{64,192},{128,0},{192,64},{1,129},{65,193},{129,1},{193,65... | collective-permute-start | bytes 1179656 | tf_op jit(solution)/shard_map/ppermute | solution.py:191
  27.8 0.0 collective-permute-done.5
  27.8 0.4 collective-permute-start.4
  28.2 0.0 collective-permute-done.11
  28.2 2.4 %collective-permute-start.6 = (f32[768,128]{1,0:T(8,128)S(1)}, f32[768,128]{1,0:T(8,128)S(1)}, u32[]{:S(2)}, u32[]{:S(2)}) collective-permute-start(f32[768,128]{1,0:T(8,128)S(1)} %add.59), channel_id=1, source_target_pairs={{0,192},{64,0},{128,64},{192,128},{1,193},{65,1},{129,65},{193,129... | collective-permute-start | bytes 1179656 | tf_op jit(solution)/shard_map/ppermute | solution.py:191
  30.7 0.0 collective-permute-done.12
  30.7 2.3 %collective-permute-start.13 = (f32[4,64,128]{2,1,0:T(8,128)S(1)}, f32[4,64,128]{2,1,0:T(8,128)S(1)}, u32[]{:S(2)}, u32[]{:S(2)}) collective-permute-start(f32[4,64,128]{2,1,0:T(8,128)S(1)} %get-tuple-element.39), channel_id=1, source_target_pairs={{0,24},{8,0},{16,8},{24,16},{1,25},{9,1},{17,9},{25,17},{2,26},{10... | collective-permute-start | bytes 393224 | tf_op jit(solution)/shard_map/ppermute | solution.py:191
  32.9 1.9 %collective-permute-done.13 = f32[4,64,128]{2,1,0:T(8,128)S(1)} collective-permute-done((f32[4,64,128]{2,1,0:T(8,128)S(1)}, f32[4,64,128]{2,1,0:T(8,128)S(1)}, u32[]{:S(2)}, u32[]{:S(2)}) %collective-permute-start.13) | collective-permute-done | bytes 131104 | tf_op jit(solution)/shard_map/ppermute | solution.py:191
  34.9 0.0 collective-permute-done
  34.9 2.3 %collective-permute-done.2 = f32[768,128]{1,0:T(8,128)S(1)} collective-permute-done((f32[768,128]{1,0:T(8,128)S(1)}, f32[768,128]{1,0:T(8,128)S(1)}, u32[]{:S(2)}, u32[]{:S(2)}) %collective-permute-start.2) | collective-permute-done | bytes 393248 | tf_op jit(solution)/shard_map/ppermute | solution.py:191
  37.2 8.8 %collective-permute-done.4 = f32[768,128]{1,0:T(8,128)S(1)} collective-permute-done((f32[768,128]{1,0:T(8,128)S(1)}, f32[768,128]{1,0:T(8,128)S(1)}, u32[]{:S(2)}, u32[]{:S(2)}) %collective-permute-start.4) | collective-permute-done | bytes 393248 | tf_op jit(solution)/shard_map/ppermute | solution.py:191
  46.0 0.0 collective-permute-done.6
  46.0 0.1 add_add_fusion
  46.1 1.6 %collective-permute-start.7 = (f32[192,128]{1,0:T(8,128)S(1)}, f32[192,128]{1,0:T(8,128)S(1)}, u32[]{:S(2)}, u32[]{:S(2)}) collective-permute-start(f32[192,128]{1,0:T(8,128)S(1)} %get-tuple-element.43), channel_id=1, source_target_pairs={{0,16},{8,24},{16,0},{24,8},{1,17},{9,25},{17,1},{25,9},{2,18},{10... | collective-permute-start | bytes 294920 | tf_op jit(solution)/shard_map/ppermute | solution.py:191
  47.7 1.3 %collective-permute-start.8 = (f32[192,128]{1,0:T(8,128)S(1)}, f32[192,128]{1,0:T(8,128)S(1)}, u32[]{:S(2)}, u32[]{:S(2)}) collective-permute-start(f32[192,128]{1,0:T(8,128)S(1)} %get-tuple-element.42), channel_id=1, source_target_pairs={{0,8},{8,16},{16,24},{24,0},{1,9},{9,17},{17,25},{25,1},{2,10},{10... | collective-permute-start | bytes 294920 | tf_op jit(solution)/shard_map/ppermute | solution.py:191
  49.0 1.4 %collective-permute-start.9 = (f32[192,128]{1,0:T(8,128)S(1)}, f32[192,128]{1,0:T(8,128)S(1)}, u32[]{:S(2)}, u32[]{:S(2)}) collective-permute-start(f32[192,128]{1,0:T(8,128)S(1)} %get-tuple-element.41), channel_id=1, source_target_pairs={{0,24},{8,0},{16,8},{24,16},{1,25},{9,1},{17,9},{25,17},{2,26},{10... | collective-permute-start | bytes 294920 | tf_op jit(solution)/shard_map/ppermute | solution.py:191
  50.4 1.7 %collective-permute-start.14 = (f32[64,128]{1,0:T(8,128)S(1)}, f32[64,128]{1,0:T(8,128)S(1)}, u32[]{:S(2)}, u32[]{:S(2)}) collective-permute-start(f32[64,128]{1,0:T(8,128)S(1)} %get-tuple-element.47), channel_id=1, source_target_pairs={{0,128},{64,192},{128,0},{192,64},{1,129},{65,193},{129,1},{193,65... | collective-permute-start | bytes 98312 | tf_op jit(solution)/shard_map/ppermute | solution.py:191
  52.1 1.4 %collective-permute-start.15 = (f32[64,128]{1,0:T(8,128)S(1)}, f32[64,128]{1,0:T(8,128)S(1)}, u32[]{:S(2)}, u32[]{:S(2)}) collective-permute-start(f32[64,128]{1,0:T(8,128)S(1)} %get-tuple-element.46), channel_id=1, source_target_pairs={{0,64},{64,128},{128,192},{192,0},{1,65},{65,129},{129,193},{193,1... | collective-permute-start | bytes 98312 | tf_op jit(solution)/shard_map/ppermute | solution.py:191
  53.5 1.2 %collective-permute-done.14.refs_5_ = f32[64,128]{1,0:T(8,128)S(1)} collective-permute-done((f32[64,128]{1,0:T(8,128)S(1)}, f32[64,128]{1,0:T(8,128)S(1)}, u32[]{:S(2)}, u32[]{:S(2)}) %collective-permute-start.14) | collective-permute-done | bytes 32800 | tf_op jit(solution)/shard_map/ppermute | solution.py:191
  54.8 2.5 %collective-permute-start.16 = (f32[64,128]{1,0:T(8,128)S(1)}, f32[64,128]{1,0:T(8,128)S(1)}, u32[]{:S(2)}, u32[]{:S(2)}) collective-permute-start(f32[64,128]{1,0:T(8,128)S(1)} %get-tuple-element.45), channel_id=1, source_target_pairs={{0,192},{64,0},{128,64},{192,128},{1,193},{65,1},{129,65},{193,129... | collective-permute-start | bytes 98312 | tf_op jit(solution)/shard_map/ppermute | solution.py:191
  57.2 0.0 collective-permute-done.15.refs_6_
  57.2 1.0 %collective-permute-done.16.refs_7_ = f32[64,128]{1,0:T(8,128)S(1)} collective-permute-done((f32[64,128]{1,0:T(8,128)S(1)}, f32[64,128]{1,0:T(8,128)S(1)}, u32[]{:S(2)}, u32[]{:S(2)}) %collective-permute-start.16) | collective-permute-done | bytes 32800 | tf_op jit(solution)/shard_map/ppermute | solution.py:191
  58.3 0.0 collective-permute-done.7.refs_1_
  58.3 0.0 collective-permute-done.8.refs_2_
  58.3 0.0 collective-permute-done.9.refs_3_
  58.3 0.7 join.1
  59.0 8.2 %all-to-all-start = ((f32[8,32,128]{2,1,0:T(8,128)}), f32[8,32,128]{2,1,0:T(8,128)S(1)}, u32[]{:S(2)}, u32[]{:S(2)}) async-start(f32[8,32,128]{2,1,0:T(8,128)} %join.1), calls=%async_computation | async-start | bytes 262144 | tf_op jit(solution)/shard_map/all_to_all | solution.py:245
  67.1 0.0 copy-done
  67.1 0.0 copy-done.1
  67.1 0.2 prepare.1
  67.3 7.7 %all-to-all-done.parts_ref = f32[8,32,128]{2,1,0:T(8,128)S(1)} async-done(((f32[8,32,128]{2,1,0:T(8,128)}), f32[8,32,128]{2,1,0:T(8,128)S(1)}, u32[]{:S(2)}, u32[]{:S(2)}) %all-to-all-start) | async-done | bytes 131104 | tf_op jit(solution)/shard_map/all_to_all | solution.py:245
  75.0 0.1 gram.1
  75.2 23.0 %all_to_all.16 = f32[256,1,128]{2,1,0:T(1,128)S(1)} all-to-all(f32[256,1,128]{2,1,0:T(1,128)S(1)} %bitcast.30), channel_id=1, replica_groups=mesh['x'=4,'core'=2,'y'=4,'z'=8] {'x','core','y','z'}, dimensions={0} | all-to-all | bytes 262144 | tf_op jit(solution)/shard_map/all_to_all | solution.py:252
  98.2 0.9 tail.1
  (7 shorter events, 0.2 us)
Async XLA Ops:
  13.0 7.7 %collective-permute-start.10 = (f32[4,4,64,128]{3,2,1,0:T(8,128)S(1)}, f32[4,4,64,128]{3,2,1,0:T(8,128)S(1)}, u32[]{:S(2)}, u32[]{:S(2)}) collective-permute-start(f32[4,4,64,128]{3,2,1,0:T(8,128)S(1)} %get-tuple-element.29), channel_id=1, source_target_pairs={{0,32},{32,0},{1,33},{33,1},{2,34},{34,2},{3,35},{35,3},{4,36},{36... | collective-permute-start | bytes 1572872 | tf_op jit(solution)/shard_map/ppermute | solution.py:228
  17.5 6.2 %collective-permute-start.1 = (f32[768,128]{1,0:T(8,128)S(1)}, f32[768,128]{1,0:T(8,128)S(1)}, u32[]{:S(2)}, u32[]{:S(2)}) collective-permute-start(f32[768,128]{1,0:T(8,128)S(1)} %get-tuple-element.23), channel_id=1, source_target_pairs={{0,32},{32,0},{1,33},{33,1},{2,34},{34,2},{3,35},{35,3},{4,36},{36... | collective-permute-start | bytes 1179656 | tf_op jit(solution)/shard_map/ppermute | solution.py:221
  18.8 6.1 %collective-permute-start.3 = (f32[768,128]{1,0:T(8,128)S(1)}, f32[768,128]{1,0:T(8,128)S(1)}, u32[]{:S(2)}, u32[]{:S(2)}) collective-permute-start(f32[768,128]{1,0:T(8,128)S(1)} %get-tuple-element.25), channel_id=1, source_target_pairs={{0,32},{32,0},{1,33},{33,1},{2,34},{34,2},{3,35},{35,3},{4,36},{36... | collective-permute-start | bytes 1179656 | tf_op jit(solution)/shard_map/ppermute | solution.py:221
  20.6 7.2 %collective-permute-start.5 = (f32[768,128]{1,0:T(8,128)S(1)}, f32[768,128]{1,0:T(8,128)S(1)}, u32[]{:S(2)}, u32[]{:S(2)}) collective-permute-start(f32[768,128]{1,0:T(8,128)S(1)} %get-tuple-element.27), channel_id=1, source_target_pairs={{0,32},{32,0},{1,33},{33,1},{2,34},{34,2},{3,35},{35,3},{4,36},{36... | collective-permute-start | bytes 1179656 | tf_op jit(solution)/shard_map/ppermute | solution.py:221
  20.7 7.5 %collective-permute-start.11 = (f32[4,64,128]{2,1,0:T(8,128)S(1)}, f32[4,64,128]{2,1,0:T(8,128)S(1)}, u32[]{:S(2)}, u32[]{:S(2)}) collective-permute-start(f32[4,64,128]{2,1,0:T(8,128)S(1)} %get-tuple-element.38), channel_id=1, source_target_pairs={{0,16},{8,24},{16,0},{24,8},{1,17},{9,25},{17,1},{25,9},{2,18},{10... | collective-permute-start | bytes 393224 | tf_op jit(solution)/shard_map/ppermute | solution.py:191
  22.1 8.6 %collective-permute-start.12 = (f32[4,64,128]{2,1,0:T(8,128)S(1)}, f32[4,64,128]{2,1,0:T(8,128)S(1)}, u32[]{:S(2)}, u32[]{:S(2)}) collective-permute-start(f32[4,64,128]{2,1,0:T(8,128)S(1)} %get-tuple-element.40), channel_id=1, source_target_pairs={{0,8},{8,16},{16,24},{24,0},{1,9},{9,17},{17,25},{25,1},{2,10},{10... | collective-permute-start | bytes 393224 | tf_op jit(solution)/shard_map/ppermute | solution.py:191
  23.7 11.2 %collective-permute-start = (f32[768,128]{1,0:T(8,128)S(1)}, f32[768,128]{1,0:T(8,128)S(1)}, u32[]{:S(2)}, u32[]{:S(2)}) collective-permute-start(f32[768,128]{1,0:T(8,128)S(1)} %get-tuple-element.21), channel_id=1, source_target_pairs={{0,32},{32,0},{1,33},{33,1},{2,34},{34,2},{3,35},{35,3},{4,36},{36... | collective-permute-start | bytes 1179656 | tf_op jit(solution)/shard_map/ppermute | solution.py:221
  24.8 42.3 %copy-start = (f32[8,32,128]{2,1,0:T(8,128)S(1)}, f32[8,32,128]{2,1,0:T(8,128)}, u32[]{:S(2)}) copy-start(f32[8,32,128]{2,1,0:T(8,128)} %hist_ref.1) | copy-start | bytes 393220
  24.8 42.3 %copy-start.1 = (f32[32,128]{1,0:T(8,128)S(1)}, f32[32,128]{1,0:T(8,128)}, u32[]{:S(2)}) copy-start(f32[32,128]{1,0:T(8,128)} %den_ref.1) | copy-start | bytes 49156
  24.9 12.3 %collective-permute-start.2 = (f32[768,128]{1,0:T(8,128)S(1)}, f32[768,128]{1,0:T(8,128)S(1)}, u32[]{:S(2)}, u32[]{:S(2)}) collective-permute-start(f32[768,128]{1,0:T(8,128)S(1)} %add.55), channel_id=1, source_target_pairs={{0,128},{64,192},{128,0},{192,64},{1,129},{65,193},{129,1},{193,65... | collective-permute-start | bytes 1179656 | tf_op jit(solution)/shard_map/ppermute | solution.py:191
  27.8 18.2 %collective-permute-start.4 = (f32[768,128]{1,0:T(8,128)S(1)}, f32[768,128]{1,0:T(8,128)S(1)}, u32[]{:S(2)}, u32[]{:S(2)}) collective-permute-start(f32[768,128]{1,0:T(8,128)S(1)} %add.57), channel_id=1, source_target_pairs={{0,64},{64,128},{128,192},{192,0},{1,65},{65,129},{129,193},{193,1... | collective-permute-start | bytes 1179656 | tf_op jit(solution)/shard_map/ppermute | solution.py:191
  28.2 17.8 %collective-permute-start.6 = (f32[768,128]{1,0:T(8,128)S(1)}, f32[768,128]{1,0:T(8,128)S(1)}, u32[]{:S(2)}, u32[]{:S(2)}) collective-permute-start(f32[768,128]{1,0:T(8,128)S(1)} %add.59), channel_id=1, source_target_pairs={{0,192},{64,0},{128,64},{192,128},{1,193},{65,1},{129,65},{193,129... | collective-permute-start | bytes 1179656 | tf_op jit(solution)/shard_map/ppermute | solution.py:191
  30.7 4.2 %collective-permute-start.13 = (f32[4,64,128]{2,1,0:T(8,128)S(1)}, f32[4,64,128]{2,1,0:T(8,128)S(1)}, u32[]{:S(2)}, u32[]{:S(2)}) collective-permute-start(f32[4,64,128]{2,1,0:T(8,128)S(1)} %get-tuple-element.39), channel_id=1, source_target_pairs={{0,24},{8,0},{16,8},{24,16},{1,25},{9,1},{17,9},{25,17},{2,26},{10... | collective-permute-start | bytes 393224 | tf_op jit(solution)/shard_map/ppermute | solution.py:191
  46.1 12.1 %collective-permute-start.7 = (f32[192,128]{1,0:T(8,128)S(1)}, f32[192,128]{1,0:T(8,128)S(1)}, u32[]{:S(2)}, u32[]{:S(2)}) collective-permute-start(f32[192,128]{1,0:T(8,128)S(1)} %get-tuple-element.43), channel_id=1, source_target_pairs={{0,16},{8,24},{16,0},{24,8},{1,17},{9,25},{17,1},{25,9},{2,18},{10... | collective-permute-start | bytes 294920 | tf_op jit(solution)/shard_map/ppermute | solution.py:191
  47.7 10.6 %collective-permute-start.8 = (f32[192,128]{1,0:T(8,128)S(1)}, f32[192,128]{1,0:T(8,128)S(1)}, u32[]{:S(2)}, u32[]{:S(2)}) collective-permute-start(f32[192,128]{1,0:T(8,128)S(1)} %get-tuple-element.42), channel_id=1, source_target_pairs={{0,8},{8,16},{16,24},{24,0},{1,9},{9,17},{17,25},{25,1},{2,10},{10... | collective-permute-start | bytes 294920 | tf_op jit(solution)/shard_map/ppermute | solution.py:191
  49.0 9.2 %collective-permute-start.9 = (f32[192,128]{1,0:T(8,128)S(1)}, f32[192,128]{1,0:T(8,128)S(1)}, u32[]{:S(2)}, u32[]{:S(2)}) collective-permute-start(f32[192,128]{1,0:T(8,128)S(1)} %get-tuple-element.41), channel_id=1, source_target_pairs={{0,24},{8,0},{16,8},{24,16},{1,25},{9,1},{17,9},{25,17},{2,26},{10... | collective-permute-start | bytes 294920 | tf_op jit(solution)/shard_map/ppermute | solution.py:191
  50.4 4.4 %collective-permute-start.14 = (f32[64,128]{1,0:T(8,128)S(1)}, f32[64,128]{1,0:T(8,128)S(1)}, u32[]{:S(2)}, u32[]{:S(2)}) collective-permute-start(f32[64,128]{1,0:T(8,128)S(1)} %get-tuple-element.47), channel_id=1, source_target_pairs={{0,128},{64,192},{128,0},{192,64},{1,129},{65,193},{129,1},{193,65... | collective-permute-start | bytes 98312 | tf_op jit(solution)/shard_map/ppermute | solution.py:191
  52.1 5.1 %collective-permute-start.15 = (f32[64,128]{1,0:T(8,128)S(1)}, f32[64,128]{1,0:T(8,128)S(1)}, u32[]{:S(2)}, u32[]{:S(2)}) collective-permute-start(f32[64,128]{1,0:T(8,128)S(1)} %get-tuple-element.46), channel_id=1, source_target_pairs={{0,64},{64,128},{128,192},{192,0},{1,65},{65,129},{129,193},{193,1... | collective-permute-start | bytes 98312 | tf_op jit(solution)/shard_map/ppermute | solution.py:191
  54.8 3.5 %collective-permute-start.16 = (f32[64,128]{1,0:T(8,128)S(1)}, f32[64,128]{1,0:T(8,128)S(1)}, u32[]{:S(2)}, u32[]{:S(2)}) collective-permute-start(f32[64,128]{1,0:T(8,128)S(1)} %get-tuple-element.45), channel_id=1, source_target_pairs={{0,192},{64,0},{128,64},{192,128},{1,193},{65,1},{129,65},{193,129... | collective-permute-start | bytes 98312 | tf_op jit(solution)/shard_map/ppermute | solution.py:191
  59.0 16.1 %all-to-all-start = ((f32[8,32,128]{2,1,0:T(8,128)}), f32[8,32,128]{2,1,0:T(8,128)S(1)}, u32[]{:S(2)}, u32[]{:S(2)}) async-start(f32[8,32,128]{2,1,0:T(8,128)} %join.1), calls=%async_computation | async-start | bytes 262144 | tf_op jit(solution)/shard_map/all_to_all | solution.py:245

commit v3 on v2

--- a/solution.py
+++ b/solution.py
@@ -134,8 +134,7 @@
     message = early_ref[...]
     for l in range(HIST):
         message = gram_entry(errors, HIST - 1, l, lane, message)
-    for s in range(32):
-        message_ref[s * 8:(s + 1) * 8, :] = message
+    message_ref[...] = message
 
 
 def tail_kernel(grams_ref, update_ref, following_ref, out_ref, coef_ref):
@@ -191,6 +190,16 @@
     return lax.ppermute(value, axis, [(i, (i + distance) % 4) for i in range(4)])
 
 
+def product(a, b):
+    return lax.dot_general(
+        a,
+        b,
+        (((0,), (0,)), ((), ())),
+        precision=lax.Precision.HIGH,
+        preferred_element_type=jnp.float32,
+    )
+
+
 def step(amplitudes, integrals, denominators, history):
     block = jax.ShapeDtypeStruct((OCC, LANES), jnp.float32)
     slabs = jax.ShapeDtypeStruct((HIST - 1, OCC, LANES), jnp.float32)
@@ -208,13 +217,8 @@
         cost_estimate=pl.CostEstimate(flops=2**20, bytes_accessed=2**21, transcendentals=0),
         name="hot",
     )()
-    partial = lax.dot_general(
-        amplitudes,
-        integrals,
-        (((0,), (0,)), ((), ())),
-        precision=lax.Precision.HIGH,
-        preferred_element_type=jnp.float32,
-    )
+    partial = product(amplitudes[:PAIRS // 2], integrals[:PAIRS // 2])
+    partial = partial + product(amplitudes[PAIRS // 2:], integrals[PAIRS // 2:])
     pieces = {}
     for distance in (2, 1, 3, 0):
         sent, kept = low_piece(partial, hot, distance)
@@ -245,11 +249,13 @@
     parts = lax.all_to_all(rows, "z", 0, 0, tiled=True)
     update, message = pl.pallas_call(
         gram_kernel,
-        out_shape=(block, jax.ShapeDtypeStruct((256, LANES), jnp.float32)),
+        out_shape=(block, jax.ShapeDtypeStruct((8, LANES), jnp.float32)),
         compiler_params=SMALL,
         name="gram",
     )(parts, divisors, errors, following, early)
-    grams = lax.all_to_all(message, ("x", "core", "y", "z"), 0, 0, tiled=True)
+    message = message + lax.ppermute(message, "core", [(0, 1), (1, 0)])
+    message = jnp.broadcast_to(message, (16, 8, LANES)).reshape(16 * 8, LANES)
+    grams = lax.all_to_all(message, ("x", "y", "z"), 0, 0, tiled=True)
     extrapolated, coefficients = pl.pallas_call(
         tail_kernel,
         out_shape=(block, jax.ShapeDtypeStruct((1, HIST), jnp.float32)),

time: 99.4 us -> 98.8 us (level)
  blocking collectives: 23 us -> 17.1 us
  starting transfers between devices: 32.9 us -> 38 us
    all_to_all x1, blocking collectives: 23 us -> 17.1 us  [step(): grams = lax.all_to_all(message, ('x', 'y', 'z'), 0, 0, tiled=True)]
    ppermute x0 -> x1, starting transfers between devices: none -> 4.85 us  [step(): message = message + lax.ppermute(message, 'core', [(0, 1), (1, 0)])]
    dot_general x1 -> x2, matrix products: 10.1 us -> 9.45 us  [product(): lax.dot_general(a, b, (((0,), (0,)), ((), ())), precision=lax.Precision.H...]
  transfers between devices with their start and end apart: 18 -> 19, of which waited for: 6 -> 7; matrix products, arithmetic and copies ran while one was open for 0% -> 0% of each run, Pallas kernels for 5% -> 5%
where the time goes in v3:
time: 98.8 us; the launch traced here: 98.5 us
  starting transfers between devices  38 us (38%)
  waiting for transfers between devices  23.8 us (24%)
  blocking collectives  17.1 us (17%)
  matrix products  9.45 us (10%)
  Pallas kernels  8.94 us (9%)
    ppermute x12, starting transfers between devices, shift(): lax.ppermute(value, axis, [(i, (i + distance) % 4) for i in range(4)])  19.6 us
    all_to_all x1, blocking collectives, step(): grams = lax.all_to_all(message, ('x', 'y', 'z'), 0, 0, tiled=True)  17.1 us
    ppermute x12, waiting for transfers between devices, shift(): lax.ppermute(value, axis, [(i, (i + distance) % 4) for i in range(4)])  15.2 us
    dot_general x2, matrix products, product(): lax.dot_general(a, b, (((0,), (0,)), ((), ())), precision=lax.Precision.H...  9.45 us
    all_to_all x1, starting transfers between devices, step(): parts = lax.all_to_all(rows, 'z', 0, 0, tiled=True)  8.19 us
    all_to_all x1, waiting for transfers between devices, step(): parts = lax.all_to_all(rows, 'z', 0, 0, tiled=True)  7.74 us
    pallas_call x5, Pallas kernels, mirrored(): pl.pallas_call(kernel, out_shape=(out, out), scratch_shapes=[pltpu.VMEM(s...  6.44 us
    ppermute x5, starting transfers between devices, step(): came = lax.ppermute(sent, 'core', [(0, 1), (1, 0)])  5.37 us
  transfers between devices with their start and end apart: 19, of which 7 were waited for; matrix products, arithmetic and copies ran while one was open for 0% of the time, Pallas kernels for 5%

profile of v3, /device:TPU:1, one launch (start us, length us, event | category | flops | bytes accessed | tf_op | source)
XLA Modules:
  0.0 98.5 jit_solution(17211681130547780363)
XLA Ops:
  0.6 0.6 hot.1.refs_1_.hot_ref
  1.2 0.0 copy-start.2
  1.3 0.0 copy-start.3
  1.3 5.9 %fusion.2 = f32[1024,1024]{1,0:T(8,128)S(1)} fusion(f32[1024,1024]{1,0:T(8,128)} %param.5, f32[1024,1024]{1,0:T(8,128)} %param.4), kind=kOutput, calls=%fused_computation.3 | convolution fusion | flops 3221225472 | bytes 8388608 | tf_op jit(solution)/shard_map/dot_general | solution.py:194
  7.2 0.0 copy-done.2
  7.2 0.0 copy-done.3
  7.2 3.6 %convolution_add_fusion.refs_0_.p_ref = f32[1024,1024]{1,0:T(8,128)S(1)} fusion(f32[1024,1024]{1,0:T(8,128)S(1)} %fusion.2, f32[1024,1024]{1,0:T(8,128)S(1)} %copy-done.2, f32[1024,1024]{1,0:T(8,128)S(1)} %copy-done.3), kind=kOutput, calls=%fused_computation | convolution fusion | flops 3222274048 | bytes 12582912 | tf_op jit(solution)/shard_map/dot_general | solution.py:194
  10.7 1.6 %shard_map.63 = (f32[4,4,64,128]{3,2,1,0:T(8,128)S(1)}, f32[4,4,64,128]{3,2,1,0:T(8,128)S(1)}) custom-call(f32[1024,1024]{1,0:T(8,128)S(1)} %convolution_add_fusion.refs_0_.p_ref, bf16[1024,1024]{1,0:T(8,128)(2,1)S(1)} %hot.1.refs_1_.hot_ref), custom_call_target="tpu_custom_call" | custom-call | flops 1073741824 | bytes 5242880 | tf_op jit(solution)/shard_map/pallas_call | solution.py:84
  12.3 3.3 %collective-permute-start.10 = (f32[4,4,64,128]{3,2,1,0:T(8,128)S(1)}, f32[4,4,64,128]{3,2,1,0:T(8,128)S(1)}, u32[]{:S(2)}, u32[]{:S(2)}) collective-permute-start(f32[4,4,64,128]{3,2,1,0:T(8,128)S(1)} %get-tuple-element.29), channel_id=1, source_target_pairs={{0,32},{32,0},{1,33},{33,1},{2,34},{34,2},{3,35},{35,3},{4,36},{36... | collective-permute-start | bytes 1572872 | tf_op jit(solution)/shard_map/ppermute | solution.py:232
  15.6 1.2 %shard_map.60 = (f32[768,128]{1,0:T(8,128)S(1)}, f32[768,128]{1,0:T(8,128)S(1)}) custom-call(f32[1024,1024]{1,0:T(8,128)S(1)} %convolution_add_fusion.refs_0_.p_ref, bf16[1024,1024]{1,0:T(8,128)(2,1)S(1)} %hot.1.refs_1_.hot_ref), custom_call_target="tpu_custom_call" | custom-call | flops 1073741824 | bytes 5242880 | tf_op jit(solution)/shard_map/pallas_call | solution.py:84
  16.9 0.3 collective-permute-start.1
  17.1 1.2 %shard_map.61 = (f32[768,128]{1,0:T(8,128)S(1)}, f32[768,128]{1,0:T(8,128)S(1)}) custom-call(f32[1024,1024]{1,0:T(8,128)S(1)} %convolution_add_fusion.refs_0_.p_ref, bf16[1024,1024]{1,0:T(8,128)(2,1)S(1)} %hot.1.refs_1_.hot_ref), custom_call_target="tpu_custom_call" | custom-call | flops 1073741824 | bytes 5242880 | tf_op jit(solution)/shard_map/pallas_call | solution.py:84
  18.4 0.6 collective-permute-start.3
  18.9 1.2 %shard_map.62 = (f32[768,128]{1,0:T(8,128)S(1)}, f32[768,128]{1,0:T(8,128)S(1)}) custom-call(f32[1024,1024]{1,0:T(8,128)S(1)} %convolution_add_fusion.refs_0_.p_ref, bf16[1024,1024]{1,0:T(8,128)(2,1)S(1)} %hot.1.refs_1_.hot_ref), custom_call_target="tpu_custom_call" | custom-call | flops 1073741824 | bytes 5242880 | tf_op jit(solution)/shard_map/pallas_call | solution.py:84
  20.2 0.1 collective-permute-start.5
  20.3 0.0 collective-permute-done.10
  20.3 1.3 %collective-permute-start.11 = (f32[4,64,128]{2,1,0:T(8,128)S(1)}, f32[4,64,128]{2,1,0:T(8,128)S(1)}, u32[]{:S(2)}, u32[]{:S(2)}) collective-permute-start(f32[4,64,128]{2,1,0:T(8,128)S(1)} %get-tuple-element.38), channel_id=1, source_target_pairs={{0,16},{8,24},{16,0},{24,8},{1,17},{9,25},{17,1},{25,9},{2,18},{10... | collective-permute-start | bytes 393224 | tf_op jit(solution)/shard_map/ppermute | solution.py:190
  21.6 0.4 collective-permute-start.12
  22.0 1.2 %shard_map.59 = (f32[768,128]{1,0:T(8,128)S(1)}, f32[768,128]{1,0:T(8,128)S(1)}) custom-call(f32[1024,1024]{1,0:T(8,128)S(1)} %convolution_add_fusion.refs_0_.p_ref, bf16[1024,1024]{1,0:T(8,128)(2,1)S(1)} %hot.1.refs_1_.hot_ref), custom_call_target="tpu_custom_call" | custom-call | flops 1073741824 | bytes 5242880 | tf_op jit(solution)/shard_map/pallas_call | solution.py:84
  23.2 0.0 collective-permute-done.1
  23.2 1.1 %collective-permute-start = (f32[768,128]{1,0:T(8,128)S(1)}, f32[768,128]{1,0:T(8,128)S(1)}, u32[]{:S(2)}, u32[]{:S(2)}) collective-permute-start(f32[768,128]{1,0:T(8,128)S(1)} %get-tuple-element.21), channel_id=1, source_target_pairs={{0,32},{32,0},{1,33},{33,1},{2,34},{34,2},{3,35},{35,3},{4,36},{36... | collective-permute-start | bytes 1179656 | tf_op jit(solution)/shard_map/ppermute | solution.py:225
  24.4 0.0 copy-start
  24.4 0.0 copy-start.1
  24.4 0.0 collective-permute-done.3
  24.4 2.9 %collective-permute-start.2 = (f32[768,128]{1,0:T(8,128)S(1)}, f32[768,128]{1,0:T(8,128)S(1)}, u32[]{:S(2)}, u32[]{:S(2)}) collective-permute-start(f32[768,128]{1,0:T(8,128)S(1)} %add.62), channel_id=1, source_target_pairs={{0,128},{64,192},{128,0},{192,64},{1,129},{65,193},{129,1},{193,65... | collective-permute-start | bytes 1179656 | tf_op jit(solution)/shard_map/ppermute | solution.py:190
  27.3 0.0 collective-permute-done.5
  27.3 0.4 collective-permute-start.4
  27.8 0.0 collective-permute-done.11
  27.8 2.4 %collective-permute-start.6 = (f32[768,128]{1,0:T(8,128)S(1)}, f32[768,128]{1,0:T(8,128)S(1)}, u32[]{:S(2)}, u32[]{:S(2)}) collective-permute-start(f32[768,128]{1,0:T(8,128)S(1)} %add.66), channel_id=1, source_target_pairs={{0,192},{64,0},{128,64},{192,128},{1,193},{65,1},{129,65},{193,129... | collective-permute-start | bytes 1179656 | tf_op jit(solution)/shard_map/ppermute | solution.py:190
  30.2 0.0 collective-permute-done.12
  30.2 2.2 %collective-permute-start.13 = (f32[4,64,128]{2,1,0:T(8,128)S(1)}, f32[4,64,128]{2,1,0:T(8,128)S(1)}, u32[]{:S(2)}, u32[]{:S(2)}) collective-permute-start(f32[4,64,128]{2,1,0:T(8,128)S(1)} %get-tuple-element.39), channel_id=1, source_target_pairs={{0,24},{8,0},{16,8},{24,16},{1,25},{9,1},{17,9},{25,17},{2,26},{10... | collective-permute-start | bytes 393224 | tf_op jit(solution)/shard_map/ppermute | solution.py:190
  32.5 1.9 %collective-permute-done.13 = f32[4,64,128]{2,1,0:T(8,128)S(1)} collective-permute-done((f32[4,64,128]{2,1,0:T(8,128)S(1)}, f32[4,64,128]{2,1,0:T(8,128)S(1)}, u32[]{:S(2)}, u32[]{:S(2)}) %collective-permute-start.13) | collective-permute-done | bytes 131104 | tf_op jit(solution)/shard_map/ppermute | solution.py:190
  34.5 0.0 collective-permute-done
  34.5 2.2 %collective-permute-done.2 = f32[768,128]{1,0:T(8,128)S(1)} collective-permute-done((f32[768,128]{1,0:T(8,128)S(1)}, f32[768,128]{1,0:T(8,128)S(1)}, u32[]{:S(2)}, u32[]{:S(2)}) %collective-permute-start.2) | collective-permute-done | bytes 393248 | tf_op jit(solution)/shard_map/ppermute | solution.py:190
  36.7 8.8 %collective-permute-done.4 = f32[768,128]{1,0:T(8,128)S(1)} collective-permute-done((f32[768,128]{1,0:T(8,128)S(1)}, f32[768,128]{1,0:T(8,128)S(1)}, u32[]{:S(2)}, u32[]{:S(2)}) %collective-permute-start.4) | collective-permute-done | bytes 393248 | tf_op jit(solution)/shard_map/ppermute | solution.py:190
  45.5 0.0 collective-permute-done.6
  45.5 0.1 add_add_fusion
  45.6 1.7 %collective-permute-start.7 = (f32[192,128]{1,0:T(8,128)S(1)}, f32[192,128]{1,0:T(8,128)S(1)}, u32[]{:S(2)}, u32[]{:S(2)}) collective-permute-start(f32[192,128]{1,0:T(8,128)S(1)} %get-tuple-element.43), channel_id=1, source_target_pairs={{0,16},{8,24},{16,0},{24,8},{1,17},{9,25},{17,1},{25,9},{2,18},{10... | collective-permute-start | bytes 294920 | tf_op jit(solution)/shard_map/ppermute | solution.py:190
  47.3 1.3 %collective-permute-start.8 = (f32[192,128]{1,0:T(8,128)S(1)}, f32[192,128]{1,0:T(8,128)S(1)}, u32[]{:S(2)}, u32[]{:S(2)}) collective-permute-start(f32[192,128]{1,0:T(8,128)S(1)} %get-tuple-element.42), channel_id=1, source_target_pairs={{0,8},{8,16},{16,24},{24,0},{1,9},{9,17},{17,25},{25,1},{2,10},{10... | collective-permute-start | bytes 294920 | tf_op jit(solution)/shard_map/ppermute | solution.py:190
  48.6 1.4 %collective-permute-start.9 = (f32[192,128]{1,0:T(8,128)S(1)}, f32[192,128]{1,0:T(8,128)S(1)}, u32[]{:S(2)}, u32[]{:S(2)}) collective-permute-start(f32[192,128]{1,0:T(8,128)S(1)} %get-tuple-element.41), channel_id=1, source_target_pairs={{0,24},{8,0},{16,8},{24,16},{1,25},{9,1},{17,9},{25,17},{2,26},{10... | collective-permute-start | bytes 294920 | tf_op jit(solution)/shard_map/ppermute | solution.py:190
  50.0 1.7 %collective-permute-start.14 = (f32[64,128]{1,0:T(8,128)S(1)}, f32[64,128]{1,0:T(8,128)S(1)}, u32[]{:S(2)}, u32[]{:S(2)}) collective-permute-start(f32[64,128]{1,0:T(8,128)S(1)} %get-tuple-element.47), channel_id=1, source_target_pairs={{0,128},{64,192},{128,0},{192,64},{1,129},{65,193},{129,1},{193,65... | collective-permute-start | bytes 98312 | tf_op jit(solution)/shard_map/ppermute | solution.py:190
  51.7 1.4 %collective-permute-start.15 = (f32[64,128]{1,0:T(8,128)S(1)}, f32[64,128]{1,0:T(8,128)S(1)}, u32[]{:S(2)}, u32[]{:S(2)}) collective-permute-start(f32[64,128]{1,0:T(8,128)S(1)} %get-tuple-element.46), channel_id=1, source_target_pairs={{0,64},{64,128},{128,192},{192,0},{1,65},{65,129},{129,193},{193,1... | collective-permute-start | bytes 98312 | tf_op jit(solution)/shard_map/ppermute | solution.py:190
  53.1 1.2 %collective-permute-done.14.refs_5_ = f32[64,128]{1,0:T(8,128)S(1)} collective-permute-done((f32[64,128]{1,0:T(8,128)S(1)}, f32[64,128]{1,0:T(8,128)S(1)}, u32[]{:S(2)}, u32[]{:S(2)}) %collective-permute-start.14) | collective-permute-done | bytes 32800 | tf_op jit(solution)/shard_map/ppermute | solution.py:190
  54.3 2.5 %collective-permute-start.16 = (f32[64,128]{1,0:T(8,128)S(1)}, f32[64,128]{1,0:T(8,128)S(1)}, u32[]{:S(2)}, u32[]{:S(2)}) collective-permute-start(f32[64,128]{1,0:T(8,128)S(1)} %get-tuple-element.45), channel_id=1, source_target_pairs={{0,192},{64,0},{128,64},{192,128},{1,193},{65,1},{129,65},{193,129... | collective-permute-start | bytes 98312 | tf_op jit(solution)/shard_map/ppermute | solution.py:190
  56.8 0.0 collective-permute-done.15.refs_6_
  56.8 1.0 %collective-permute-done.16.refs_7_ = f32[64,128]{1,0:T(8,128)S(1)} collective-permute-done((f32[64,128]{1,0:T(8,128)S(1)}, f32[64,128]{1,0:T(8,128)S(1)}, u32[]{:S(2)}, u32[]{:S(2)}) %collective-permute-start.16) | collective-permute-done | bytes 32800 | tf_op jit(solution)/shard_map/ppermute | solution.py:190
  57.8 0.0 collective-permute-done.7.refs_1_
  57.8 0.0 collective-permute-done.8.refs_2_
  57.8 0.0 collective-permute-done.9.refs_3_
  57.8 0.7 join.1
  58.5 8.2 %all-to-all-start = ((f32[8,32,128]{2,1,0:T(8,128)}), f32[8,32,128]{2,1,0:T(8,128)S(1)}, u32[]{:S(2)}, u32[]{:S(2)}) async-start(f32[8,32,128]{2,1,0:T(8,128)} %join.1), calls=%async_computation | async-start | bytes 262144 | tf_op jit(solution)/shard_map/all_to_all | solution.py:249
  66.7 0.0 copy-done
  66.7 0.0 copy-done.1
  66.7 0.2 prepare.1
  66.9 7.7 %all-to-all-done.parts_ref = f32[8,32,128]{2,1,0:T(8,128)S(1)} async-done(((f32[8,32,128]{2,1,0:T(8,128)}), f32[8,32,128]{2,1,0:T(8,128)S(1)}, u32[]{:S(2)}, u32[]{:S(2)}) %all-to-all-start) | async-done | bytes 131104 | tf_op jit(solution)/shard_map/all_to_all | solution.py:249
  74.6 0.1 gram.1
  74.8 4.9 %collective-permute-start.17 = (f32[8,128]{1,0:T(8,128)S(1)}, f32[8,128]{1,0:T(8,128)S(1)}, u32[]{:S(2)}, u32[]{:S(2)}) collective-permute-start(f32[8,128]{1,0:T(8,128)S(1)} %get-tuple-element.34), channel_id=1, source_target_pairs={{0,32},{32,0},{1,33},{33,1},{2,34},{34,2},{3,35},{35,3},{4,36},{36... | collective-permute-start | bytes 12296 | tf_op jit(solution)/shard_map/ppermute | solution.py:256
  79.6 0.8 collective-permute-done.17
  80.5 17.1 %all_to_all.16 = f32[128,1,128]{2,1,0:T(1,128)S(1)} all-to-all(f32[128,1,128]{2,1,0:T(1,128)S(1)} %bitcast.26), channel_id=1, replica_groups=mesh['x'=4,'core'=2,'y'=4,'z'=8] {'x','y','z'}, dimensions={0} | all-to-all | bytes 131072 | tf_op jit(solution)/shard_map/all_to_all | solution.py:258
  97.6 0.9 tail.1
  (9 shorter events, 0.3 us)
Async XLA Ops:
  1.2 5.9 %copy-start.2 = (f32[1024,1024]{1,0:T(8,128)S(1)}, f32[1024,1024]{1,0:T(8,128)}, u32[]{:S(2)}) copy-start(f32[1024,1024]{1,0:T(8,128)} %param.5) | copy-start | bytes 12582916
  1.3 5.9 %copy-start.3 = (f32[1024,1024]{1,0:T(8,128)S(1)}, f32[1024,1024]{1,0:T(8,128)}, u32[]{:S(2)}) copy-start(f32[1024,1024]{1,0:T(8,128)} %param.4) | copy-start | bytes 12582916
  12.3 7.9 %collective-permute-start.10 = (f32[4,4,64,128]{3,2,1,0:T(8,128)S(1)}, f32[4,4,64,128]{3,2,1,0:T(8,128)S(1)}, u32[]{:S(2)}, u32[]{:S(2)}) collective-permute-start(f32[4,4,64,128]{3,2,1,0:T(8,128)S(1)} %get-tuple-element.29), channel_id=1, source_target_pairs={{0,32},{32,0},{1,33},{33,1},{2,34},{34,2},{3,35},{35,3},{4,36},{36... | collective-permute-start | bytes 1572872 | tf_op jit(solution)/shard_map/ppermute | solution.py:232
  16.9 6.4 %collective-permute-start.1 = (f32[768,128]{1,0:T(8,128)S(1)}, f32[768,128]{1,0:T(8,128)S(1)}, u32[]{:S(2)}, u32[]{:S(2)}) collective-permute-start(f32[768,128]{1,0:T(8,128)S(1)} %get-tuple-element.23), channel_id=1, source_target_pairs={{0,32},{32,0},{1,33},{33,1},{2,34},{34,2},{3,35},{35,3},{4,36},{36... | collective-permute-start | bytes 1179656 | tf_op jit(solution)/shard_map/ppermute | solution.py:225
  18.4 6.0 %collective-permute-start.3 = (f32[768,128]{1,0:T(8,128)S(1)}, f32[768,128]{1,0:T(8,128)S(1)}, u32[]{:S(2)}, u32[]{:S(2)}) collective-permute-start(f32[768,128]{1,0:T(8,128)S(1)} %get-tuple-element.25), channel_id=1, source_target_pairs={{0,32},{32,0},{1,33},{33,1},{2,34},{34,2},{3,35},{35,3},{4,36},{36... | collective-permute-start | bytes 1179656 | tf_op jit(solution)/shard_map/ppermute | solution.py:225
  20.2 7.2 %collective-permute-start.5 = (f32[768,128]{1,0:T(8,128)S(1)}, f32[768,128]{1,0:T(8,128)S(1)}, u32[]{:S(2)}, u32[]{:S(2)}) collective-permute-start(f32[768,128]{1,0:T(8,128)S(1)} %get-tuple-element.27), channel_id=1, source_target_pairs={{0,32},{32,0},{1,33},{33,1},{2,34},{34,2},{3,35},{35,3},{4,36},{36... | collective-permute-start | bytes 1179656 | tf_op jit(solution)/shard_map/ppermute | solution.py:225
  20.3 7.5 %collective-permute-start.11 = (f32[4,64,128]{2,1,0:T(8,128)S(1)}, f32[4,64,128]{2,1,0:T(8,128)S(1)}, u32[]{:S(2)}, u32[]{:S(2)}) collective-permute-start(f32[4,64,128]{2,1,0:T(8,128)S(1)} %get-tuple-element.38), channel_id=1, source_target_pairs={{0,16},{8,24},{16,0},{24,8},{1,17},{9,25},{17,1},{25,9},{2,18},{10... | collective-permute-start | bytes 393224 | tf_op jit(solution)/shard_map/ppermute | solution.py:190
  21.6 8.6 %collective-permute-start.12 = (f32[4,64,128]{2,1,0:T(8,128)S(1)}, f32[4,64,128]{2,1,0:T(8,128)S(1)}, u32[]{:S(2)}, u32[]{:S(2)}) collective-permute-start(f32[4,64,128]{2,1,0:T(8,128)S(1)} %get-tuple-element.40), channel_id=1, source_target_pairs={{0,8},{8,16},{16,24},{24,0},{1,9},{9,17},{17,25},{25,1},{2,10},{10... | collective-permute-start | bytes 393224 | tf_op jit(solution)/shard_map/ppermute | solution.py:190
  23.2 11.2 %collective-permute-start = (f32[768,128]{1,0:T(8,128)S(1)}, f32[768,128]{1,0:T(8,128)S(1)}, u32[]{:S(2)}, u32[]{:S(2)}) collective-permute-start(f32[768,128]{1,0:T(8,128)S(1)} %get-tuple-element.21), channel_id=1, source_target_pairs={{0,32},{32,0},{1,33},{33,1},{2,34},{34,2},{3,35},{35,3},{4,36},{36... | collective-permute-start | bytes 1179656 | tf_op jit(solution)/shard_map/ppermute | solution.py:225
  24.4 42.3 %copy-start = (f32[8,32,128]{2,1,0:T(8,128)S(1)}, f32[8,32,128]{2,1,0:T(8,128)}, u32[]{:S(2)}) copy-start(f32[8,32,128]{2,1,0:T(8,128)} %hist_ref.1) | copy-start | bytes 393220
  24.4 42.3 %copy-start.1 = (f32[32,128]{1,0:T(8,128)S(1)}, f32[32,128]{1,0:T(8,128)}, u32[]{:S(2)}) copy-start(f32[32,128]{1,0:T(8,128)} %den_ref.1) | copy-start | bytes 49156
  24.4 12.3 %collective-permute-start.2 = (f32[768,128]{1,0:T(8,128)S(1)}, f32[768,128]{1,0:T(8,128)S(1)}, u32[]{:S(2)}, u32[]{:S(2)}) collective-permute-start(f32[768,128]{1,0:T(8,128)S(1)} %add.62), channel_id=1, source_target_pairs={{0,128},{64,192},{128,0},{192,64},{1,129},{65,193},{129,1},{193,65... | collective-permute-start | bytes 1179656 | tf_op jit(solution)/shard_map/ppermute | solution.py:190
  27.3 18.2 %collective-permute-start.4 = (f32[768,128]{1,0:T(8,128)S(1)}, f32[768,128]{1,0:T(8,128)S(1)}, u32[]{:S(2)}, u32[]{:S(2)}) collective-permute-start(f32[768,128]{1,0:T(8,128)S(1)} %add.64), channel_id=1, source_target_pairs={{0,64},{64,128},{128,192},{192,0},{1,65},{65,129},{129,193},{193,1... | collective-permute-start | bytes 1179656 | tf_op jit(solution)/shard_map/ppermute | solution.py:190
  27.8 17.7 %collective-permute-start.6 = (f32[768,128]{1,0:T(8,128)S(1)}, f32[768,128]{1,0:T(8,128)S(1)}, u32[]{:S(2)}, u32[]{:S(2)}) collective-permute-start(f32[768,128]{1,0:T(8,128)S(1)} %add.66), channel_id=1, source_target_pairs={{0,192},{64,0},{128,64},{192,128},{1,193},{65,1},{129,65},{193,129... | collective-permute-start | bytes 1179656 | tf_op jit(solution)/shard_map/ppermute | solution.py:190
  30.2 4.2 %collective-permute-start.13 = (f32[4,64,128]{2,1,0:T(8,128)S(1)}, f32[4,64,128]{2,1,0:T(8,128)S(1)}, u32[]{:S(2)}, u32[]{:S(2)}) collective-permute-start(f32[4,64,128]{2,1,0:T(8,128)S(1)} %get-tuple-element.39), channel_id=1, source_target_pairs={{0,24},{8,0},{16,8},{24,16},{1,25},{9,1},{17,9},{25,17},{2,26},{10... | collective-permute-start | bytes 393224 | tf_op jit(solution)/shard_map/ppermute | solution.py:190
  45.6 12.2 %collective-permute-start.7 = (f32[192,128]{1,0:T(8,128)S(1)}, f32[192,128]{1,0:T(8,128)S(1)}, u32[]{:S(2)}, u32[]{:S(2)}) collective-permute-start(f32[192,128]{1,0:T(8,128)S(1)} %get-tuple-element.43), channel_id=1, source_target_pairs={{0,16},{8,24},{16,0},{24,8},{1,17},{9,25},{17,1},{25,9},{2,18},{10... | collective-permute-start | bytes 294920 | tf_op jit(solution)/shard_map/ppermute | solution.py:190
  47.3 10.5 %collective-permute-start.8 = (f32[192,128]{1,0:T(8,128)S(1)}, f32[192,128]{1,0:T(8,128)S(1)}, u32[]{:S(2)}, u32[]{:S(2)}) collective-permute-start(f32[192,128]{1,0:T(8,128)S(1)} %get-tuple-element.42), channel_id=1, source_target_pairs={{0,8},{8,16},{16,24},{24,0},{1,9},{9,17},{17,25},{25,1},{2,10},{10... | collective-permute-start | bytes 294920 | tf_op jit(solution)/shard_map/ppermute | solution.py:190
  48.6 9.2 %collective-permute-start.9 = (f32[192,128]{1,0:T(8,128)S(1)}, f32[192,128]{1,0:T(8,128)S(1)}, u32[]{:S(2)}, u32[]{:S(2)}) collective-permute-start(f32[192,128]{1,0:T(8,128)S(1)} %get-tuple-element.41), channel_id=1, source_target_pairs={{0,24},{8,0},{16,8},{24,16},{1,25},{9,1},{17,9},{25,17},{2,26},{10... | collective-permute-start | bytes 294920 | tf_op jit(solution)/shard_map/ppermute | solution.py:190
  50.0 4.4 %collective-permute-start.14 = (f32[64,128]{1,0:T(8,128)S(1)}, f32[64,128]{1,0:T(8,128)S(1)}, u32[]{:S(2)}, u32[]{:S(2)}) collective-permute-start(f32[64,128]{1,0:T(8,128)S(1)} %get-tuple-element.47), channel_id=1, source_target_pairs={{0,128},{64,192},{128,0},{192,64},{1,129},{65,193},{129,1},{193,65... | collective-permute-start | bytes 98312 | tf_op jit(solution)/shard_map/ppermute | solution.py:190
  51.7 5.1 %collective-permute-start.15 = (f32[64,128]{1,0:T(8,128)S(1)}, f32[64,128]{1,0:T(8,128)S(1)}, u32[]{:S(2)}, u32[]{:S(2)}) collective-permute-start(f32[64,128]{1,0:T(8,128)S(1)} %get-tuple-element.46), channel_id=1, source_target_pairs={{0,64},{64,128},{128,192},{192,0},{1,65},{65,129},{129,193},{193,1... | collective-permute-start | bytes 98312 | tf_op jit(solution)/shard_map/ppermute | solution.py:190
  54.3 3.5 %collective-permute-start.16 = (f32[64,128]{1,0:T(8,128)S(1)}, f32[64,128]{1,0:T(8,128)S(1)}, u32[]{:S(2)}, u32[]{:S(2)}) collective-permute-start(f32[64,128]{1,0:T(8,128)S(1)} %get-tuple-element.45), channel_id=1, source_target_pairs={{0,192},{64,0},{128,64},{192,128},{1,193},{65,1},{129,65},{193,129... | collective-permute-start | bytes 98312 | tf_op jit(solution)/shard_map/ppermute | solution.py:190
  58.5 16.1 %all-to-all-start = ((f32[8,32,128]{2,1,0:T(8,128)}), f32[8,32,128]{2,1,0:T(8,128)S(1)}, u32[]{:S(2)}, u32[]{:S(2)}) async-start(f32[8,32,128]{2,1,0:T(8,128)} %join.1), calls=%async_computation | async-start | bytes 262144 | tf_op jit(solution)/shard_map/all_to_all | solution.py:249
  74.8 5.7 %collective-permute-start.17 = (f32[8,128]{1,0:T(8,128)S(1)}, f32[8,128]{1,0:T(8,128)S(1)}, u32[]{:S(2)}, u32[]{:S(2)}) collective-permute-start(f32[8,128]{1,0:T(8,128)S(1)} %get-tuple-element.34), channel_id=1, source_target_pairs={{0,32},{32,0},{1,33},{33,1},{2,34},{34,2},{3,35},{35,3},{4,36},{36... | collective-permute-start | bytes 12296 | tf_op jit(solution)/shard_map/ppermute | solution.py:256

commit v4 on v1

--- a/solution.py
+++ b/solution.py
@@ -191,6 +191,16 @@
     return lax.ppermute(value, axis, [(i, (i + distance) % 4) for i in range(4)])
 
 
+def product(a, b):
+    return lax.dot_general(
+        a,
+        b,
+        (((0,), (0,)), ((), ())),
+        precision=lax.Precision.HIGH,
+        preferred_element_type=jnp.float32,
+    )
+
+
 def step(amplitudes, integrals, denominators, history):
     block = jax.ShapeDtypeStruct((OCC, LANES), jnp.float32)
     slabs = jax.ShapeDtypeStruct((HIST - 1, OCC, LANES), jnp.float32)
@@ -208,13 +218,8 @@
         cost_estimate=pl.CostEstimate(flops=2**20, bytes_accessed=2**21, transcendentals=0),
         name="hot",
     )()
-    partial = lax.dot_general(
-        amplitudes,
-        integrals,
-        (((0,), (0,)), ((), ())),
-        precision=lax.Precision.HIGH,
-        preferred_element_type=jnp.float32,
-    )
+    partial = product(amplitudes[:PAIRS // 2], integrals[:PAIRS // 2])
+    partial = partial + product(amplitudes[PAIRS // 2:], integrals[PAIRS // 2:])
     pieces = {}
     for distance in (2, 1, 3, 0):
         sent, kept = low_piece(partial, hot, distance)
@@ -246,8 +251,13 @@
     for e in (2, 1, 3):
         high = high + shift(kept[e] + came[e], "y", e)
     low = [piece for h in range(2) for piece in lows[h].reshape(2, 8 * LOW, LANES)]
-    parts = [low[0]] + [shift(low[e], "y", e) for e in (2, 1, 3)]
-    parts += [high[0]] + [shift(high[d], "x", d) for d in (2, 1, 3)]
+    quarters = [high[0]]
+    for d in (2, 1, 3):
+        quarters.append(shift(high[d], "x", d))
+    parts = [low[0]]
+    for e in (2, 1, 3):
+        parts.append(shift(low[e], "y", e))
+    parts += quarters
     rows = pl.pallas_call(
         join_kernel,
         out_shape=jax.ShapeDtypeStruct((8, OCC, LANES), jnp.float32),

time: 98.6 us -> 98 us (level)
    dot_general x1 -> x2, matrix products: 10.1 us -> 9.45 us  [product(): lax.dot_general(a, b, (((0,), (0,)), ((), ())), precision=lax.Precision.H...]
where the time goes in v4:
time: 98 us; the launch traced here: 97.8 us
  starting transfers between devices  30.9 us (32%)
  blocking collectives  24.4 us (25%)
  waiting for transfers between devices  22.8 us (23%)
  matrix products  9.45 us (10%)
  Pallas kernels  8.95 us (9%)
    all_to_all x1, blocking collectives, step(): grams = lax.all_to_all(message, ('x', 'core', 'y', 'z'), 0, 0, tiled=True)  24.4 us
    ppermute x15, starting transfers between devices, shift(): lax.ppermute(value, axis, [(i, (i + distance) % 4) for i in range(4)])  18 us
    ppermute x15, waiting for transfers between devices, shift(): lax.ppermute(value, axis, [(i, (i + distance) % 4) for i in range(4)])  15 us
    dot_general x2, matrix products, product(): lax.dot_general(a, b, (((0,), (0,)), ((), ())), precision=lax.Precision.H...  9.45 us
    all_to_all x1, starting transfers between devices, step(): parts = lax.all_to_all(rows, 'z', 0, 0, tiled=True)  8.11 us
    all_to_all x1, waiting for transfers between devices, step(): parts = lax.all_to_all(rows, 'z', 0, 0, tiled=True)  7.74 us
    pallas_call x5, Pallas kernels, mirrored(): pl.pallas_call(kernel, out_shape=(out, out), scratch_shapes=[pltpu.VMEM(s...  6.44 us
    ppermute x5, starting transfers between devices, step(): came = lax.ppermute(sent, 'core', [(0, 1), (1, 0)])  4.83 us
  transfers between devices with their start and end apart: 21, of which 7 were waited for; matrix products, arithmetic and copies ran while one was open for 0% of the time, Pallas kernels for 5%

profile of v4, /device:TPU:1, one launch (start us, length us, event | category | flops | bytes accessed | tf_op | source)
XLA Modules:
  0.0 97.8 jit_solution(3219138908541486694)
XLA Ops:
  0.6 0.6 hot.1.refs_1_.hot_ref
  1.2 0.0 copy-start.2
  1.3 0.0 copy-start.3
  1.3 5.9 %fusion.2 = f32[1024,1024]{1,0:T(8,128)S(1)} fusion(f32[1024,1024]{1,0:T(8,128)} %param.5, f32[1024,1024]{1,0:T(8,128)} %param.4), kind=kOutput, calls=%fused_computation.3 | convolution fusion | flops 3221225472 | bytes 8388608 | tf_op jit(solution)/shard_map/dot_general | solution.py:195
  7.2 0.0 copy-done.2
  7.2 0.0 copy-done.3
  7.2 3.6 %convolution_add_fusion.refs_0_.p_ref = f32[1024,1024]{1,0:T(8,128)S(1)} fusion(f32[1024,1024]{1,0:T(8,128)S(1)} %fusion.2, f32[1024,1024]{1,0:T(8,128)S(1)} %copy-done.2, f32[1024,1024]{1,0:T(8,128)S(1)} %copy-done.3), kind=kOutput, calls=%fused_computation | convolution fusion | flops 3222274048 | bytes 12582912 | tf_op jit(solution)/shard_map/dot_general | solution.py:195
  10.7 1.2 %shard_map.61 = (f32[768,128]{1,0:T(8,128)S(1)}, f32[768,128]{1,0:T(8,128)S(1)}) custom-call(f32[1024,1024]{1,0:T(8,128)S(1)} %convolution_add_fusion.refs_0_.p_ref, bf16[1024,1024]{1,0:T(8,128)(2,1)S(1)} %hot.1.refs_1_.hot_ref), custom_call_target="tpu_custom_call" | custom-call | flops 1073741824 | bytes 5242880 | tf_op jit(solution)/shard_map/pallas_call | solution.py:84
  12.0 3.3 %collective-permute-start.2 = (f32[768,128]{1,0:T(8,128)S(1)}, f32[768,128]{1,0:T(8,128)S(1)}, u32[]{:S(2)}, u32[]{:S(2)}) collective-permute-start(f32[768,128]{1,0:T(8,128)S(1)} %get-tuple-element.31), channel_id=1, source_target_pairs={{0,32},{32,0},{1,33},{33,1},{2,34},{34,2},{3,35},{35,3},{4,36},{36... | collective-permute-start | bytes 1179656 | tf_op jit(solution)/shard_map/ppermute | solution.py:226
  15.3 1.2 %shard_map.60 = (f32[768,128]{1,0:T(8,128)S(1)}, f32[768,128]{1,0:T(8,128)S(1)}) custom-call(f32[1024,1024]{1,0:T(8,128)S(1)} %convolution_add_fusion.refs_0_.p_ref, bf16[1024,1024]{1,0:T(8,128)(2,1)S(1)} %hot.1.refs_1_.hot_ref), custom_call_target="tpu_custom_call" | custom-call | flops 1073741824 | bytes 5242880 | tf_op jit(solution)/shard_map/pallas_call | solution.py:84
  16.5 0.1 collective-permute-start.1
  16.6 1.2 %shard_map.62 = (f32[768,128]{1,0:T(8,128)S(1)}, f32[768,128]{1,0:T(8,128)S(1)}) custom-call(f32[1024,1024]{1,0:T(8,128)S(1)} %convolution_add_fusion.refs_0_.p_ref, bf16[1024,1024]{1,0:T(8,128)(2,1)S(1)} %hot.1.refs_1_.hot_ref), custom_call_target="tpu_custom_call" | custom-call | flops 1073741824 | bytes 5242880 | tf_op jit(solution)/shard_map/pallas_call | solution.py:84
  17.8 0.7 collective-permute-start.5
  18.6 1.2 %shard_map.59 = (f32[768,128]{1,0:T(8,128)S(1)}, f32[768,128]{1,0:T(8,128)S(1)}) custom-call(f32[1024,1024]{1,0:T(8,128)S(1)} %convolution_add_fusion.refs_0_.p_ref, bf16[1024,1024]{1,0:T(8,128)(2,1)S(1)} %hot.1.refs_1_.hot_ref), custom_call_target="tpu_custom_call" | custom-call | flops 1073741824 | bytes 5242880 | tf_op jit(solution)/shard_map/pallas_call | solution.py:84
  19.8 0.1 collective-permute-start
  19.9 1.6 %shard_map.63 = (f32[4,4,64,128]{3,2,1,0:T(8,128)S(1)}, f32[4,4,64,128]{3,2,1,0:T(8,128)S(1)}) custom-call(f32[1024,1024]{1,0:T(8,128)S(1)} %convolution_add_fusion.refs_0_.p_ref, bf16[1024,1024]{1,0:T(8,128)(2,1)S(1)} %hot.1.refs_1_.hot_ref), custom_call_target="tpu_custom_call" | custom-call | flops 1073741824 | bytes 5242880 | tf_op jit(solution)/shard_map/pallas_call | solution.py:84
  21.5 0.6 collective-permute-start.13
  22.1 0.0 collective-permute-done.2
  22.1 0.1 collective-permute-start.3
  22.2 0.0 collective-permute-done.5
  22.2 2.7 %collective-permute-start.8 = (f32[384,128]{1,0:T(8,128)S(1)}, f32[384,128]{1,0:T(8,128)S(1)}, u32[]{:S(2)}, u32[]{:S(2)}) collective-permute-start(f32[384,128]{1,0:T(8,128)S(1)} %get-tuple-element.55), channel_id=1, source_target_pairs={{0,192},{64,0},{128,64},{192,128},{1,193},{65,1},{129,65},{193,129... | collective-permute-start | bytes 589832 | tf_op jit(solution)/shard_map/ppermute | solution.py:191
  24.9 0.0 copy-start
  24.9 0.0 collective-permute-done.1
  24.9 0.1 collective-permute-start.6
  25.0 0.0 collective-permute-done.13
  25.0 0.1 fusion.9
  25.1 2.5 %collective-permute-start.14 = (f32[4,64,128]{2,1,0:T(8,128)S(1)}, f32[4,64,128]{2,1,0:T(8,128)S(1)}, u32[]{:S(2)}, u32[]{:S(2)}) collective-permute-start(f32[4,64,128]{2,1,0:T(8,128)S(1)} %get-tuple-element.50), channel_id=1, source_target_pairs={{0,16},{8,24},{16,0},{24,8},{1,17},{9,25},{17,1},{25,9},{2,18},{10... | collective-permute-start | bytes 393224 | tf_op jit(solution)/shard_map/ppermute | solution.py:191
  27.6 2.2 %collective-permute-done.3 = f32[384,128]{1,0:T(8,128)S(1)} collective-permute-done((f32[384,128]{1,0:T(8,128)S(1)}, f32[384,128]{1,0:T(8,128)S(1)}, u32[]{:S(2)}, u32[]{:S(2)}) %collective-permute-start.3) | collective-permute-done | bytes 196640 | tf_op jit(solution)/shard_map/ppermute | solution.py:191
  29.8 0.0 collective-permute-start.15
  29.8 0.0 collective-permute-done.8
  29.8 2.7 %collective-permute-start.16 = (f32[4,64,128]{2,1,0:T(8,128)S(1)}, f32[4,64,128]{2,1,0:T(8,128)S(1)}, u32[]{:S(2)}, u32[]{:S(2)}) collective-permute-start(f32[4,64,128]{2,1,0:T(8,128)S(1)} %get-tuple-element.51), channel_id=1, source_target_pairs={{0,24},{8,0},{16,8},{24,16},{1,25},{9,1},{17,9},{25,17},{2,26},{10... | collective-permute-start | bytes 393224 | tf_op jit(solution)/shard_map/ppermute | solution.py:191
  32.6 0.0 collective-permute-done.14
  32.6 0.1 collective-permute-start.7
  32.7 2.5 %collective-permute-done.15 = f32[4,64,128]{2,1,0:T(8,128)S(1)} collective-permute-done((f32[4,64,128]{2,1,0:T(8,128)S(1)}, f32[4,64,128]{2,1,0:T(8,128)S(1)}, u32[]{:S(2)}, u32[]{:S(2)}) %collective-permute-start.15) | collective-permute-done | bytes 131104 | tf_op jit(solution)/shard_map/ppermute | solution.py:191
  35.2 1.0 collective-permute-start.4
  36.2 0.0 collective-permute-done.16
  36.2 1.7 %collective-permute-start.9 = (f32[384,128]{1,0:T(8,128)S(1)}, f32[384,128]{1,0:T(8,128)S(1)}, u32[]{:S(2)}, u32[]{:S(2)}) collective-permute-start(f32[384,128]{1,0:T(8,128)S(1)} %add_add_fusion), channel_id=1, source_target_pairs={{0,192},{64,0},{128,64},{192,128},{1,193},{65,1},{129,65},{193,129... | collective-permute-start | bytes 589832 | tf_op jit(solution)/shard_map/ppermute | solution.py:191
  37.9 0.0 collective-permute-done
  37.9 0.0 collective-permute-done.6
  38.0 0.9 collective-permute-done.7
  38.9 4.4 %collective-permute-done.4 = f32[384,128]{1,0:T(8,128)S(1)} collective-permute-done((f32[384,128]{1,0:T(8,128)S(1)}, f32[384,128]{1,0:T(8,128)S(1)}, u32[]{:S(2)}, u32[]{:S(2)}) %collective-permute-start.4) | collective-permute-done | bytes 196640 | tf_op jit(solution)/shard_map/ppermute | solution.py:191
  43.3 0.0 collective-permute-done.9
  43.3 0.1 fusion.5
  43.4 1.8 %collective-permute-start.10 = (f32[192,128]{1,0:T(8,128)S(1)}, f32[192,128]{1,0:T(8,128)S(1)}, u32[]{:S(2)}, u32[]{:S(2)}) collective-permute-start(f32[192,128]{1,0:T(8,128)S(1)} %get-tuple-element.58), channel_id=1, source_target_pairs={{0,16},{8,24},{16,0},{24,8},{1,17},{9,25},{17,1},{25,9},{2,18},{10... | collective-permute-start | bytes 294920 | tf_op jit(solution)/shard_map/ppermute | solution.py:191
  45.3 0.1 collective-permute-start.11
  45.4 2.7 %collective-permute-start.12 = (f32[192,128]{1,0:T(8,128)S(1)}, f32[192,128]{1,0:T(8,128)S(1)}, u32[]{:S(2)}, u32[]{:S(2)}) collective-permute-start(f32[192,128]{1,0:T(8,128)S(1)} %get-tuple-element.57), channel_id=1, source_target_pairs={{0,24},{8,0},{16,8},{24,16},{1,25},{9,1},{17,9},{25,17},{2,26},{10... | collective-permute-start | bytes 294920 | tf_op jit(solution)/shard_map/ppermute | solution.py:191
  48.0 0.1 collective-permute-start.17
  48.1 1.6 %collective-permute-start.18 = (f32[64,128]{1,0:T(8,128)S(1)}, f32[64,128]{1,0:T(8,128)S(1)}, u32[]{:S(2)}, u32[]{:S(2)}) collective-permute-start(f32[64,128]{1,0:T(8,128)S(1)} %get-tuple-element.62), channel_id=1, source_target_pairs={{0,64},{64,128},{128,192},{192,0},{1,65},{65,129},{129,193},{193,1... | collective-permute-start | bytes 98312 | tf_op jit(solution)/shard_map/ppermute | solution.py:191
  49.7 2.8 %collective-permute-done.17.refs_5_ = f32[64,128]{1,0:T(8,128)S(1)} collective-permute-done((f32[64,128]{1,0:T(8,128)S(1)}, f32[64,128]{1,0:T(8,128)S(1)}, u32[]{:S(2)}, u32[]{:S(2)}) %collective-permute-start.17) | collective-permute-done | bytes 32800 | tf_op jit(solution)/shard_map/ppermute | solution.py:191
  52.5 0.9 collective-permute-start.19
  53.4 0.0 collective-permute-done.18.refs_6_
  53.4 2.1 %collective-permute-done.19.refs_7_ = f32[64,128]{1,0:T(8,128)S(1)} collective-permute-done((f32[64,128]{1,0:T(8,128)S(1)}, f32[64,128]{1,0:T(8,128)S(1)}, u32[]{:S(2)}, u32[]{:S(2)}) %collective-permute-start.19) | collective-permute-done | bytes 32800 | tf_op jit(solution)/shard_map/ppermute | solution.py:191
  55.6 0.0 collective-permute-done.10.refs_1_
  55.6 0.0 collective-permute-done.11.refs_2_
  55.6 0.0 collective-permute-done.12.refs_3_
  55.6 0.7 join.1
  56.2 8.1 %all-to-all-start = ((f32[8,32,128]{2,1,0:T(8,128)}), f32[8,32,128]{2,1,0:T(8,128)S(1)}, u32[]{:S(2)}, u32[]{:S(2)}) async-start(f32[8,32,128]{2,1,0:T(8,128)} %join.1), calls=%async_computation | async-start | bytes 262144 | tf_op jit(solution)/shard_map/all_to_all | solution.py:267
  64.4 0.0 copy-done
  64.4 0.0 copy-done.1
  64.4 0.2 prepare.1
  64.5 7.7 %all-to-all-done.parts_ref = f32[8,32,128]{2,1,0:T(8,128)S(1)} async-done(((f32[8,32,128]{2,1,0:T(8,128)}), f32[8,32,128]{2,1,0:T(8,128)S(1)}, u32[]{:S(2)}, u32[]{:S(2)}) %all-to-all-start) | async-done | bytes 131104 | tf_op jit(solution)/shard_map/all_to_all | solution.py:267
  72.3 0.1 gram.1
  72.4 24.4 %all_to_all.16 = f32[256,1,128]{2,1,0:T(1,128)S(1)} all-to-all(f32[256,1,128]{2,1,0:T(1,128)S(1)} %bitcast.28), channel_id=1, replica_groups=mesh['x'=4,'core'=2,'y'=4,'z'=8] {'x','core','y','z'}, dimensions={0} | all-to-all | bytes 262144 | tf_op jit(solution)/shard_map/all_to_all | solution.py:274
  96.8 0.9 tail.1
  (10 shorter events, 0.2 us)
Async XLA Ops:
  1.2 5.9 %copy-start.2 = (f32[1024,1024]{1,0:T(8,128)S(1)}, f32[1024,1024]{1,0:T(8,128)}, u32[]{:S(2)}) copy-start(f32[1024,1024]{1,0:T(8,128)} %param.5) | copy-start | bytes 12582916
  1.3 5.9 %copy-start.3 = (f32[1024,1024]{1,0:T(8,128)S(1)}, f32[1024,1024]{1,0:T(8,128)}, u32[]{:S(2)}) copy-start(f32[1024,1024]{1,0:T(8,128)} %param.4) | copy-start | bytes 12582916
  12.0 10.1 %collective-permute-start.2 = (f32[768,128]{1,0:T(8,128)S(1)}, f32[768,128]{1,0:T(8,128)S(1)}, u32[]{:S(2)}, u32[]{:S(2)}) collective-permute-start(f32[768,128]{1,0:T(8,128)S(1)} %get-tuple-element.31), channel_id=1, source_target_pairs={{0,32},{32,0},{1,33},{33,1},{2,34},{34,2},{3,35},{35,3},{4,36},{36... | collective-permute-start | bytes 1179656 | tf_op jit(solution)/shard_map/ppermute | solution.py:226
  16.5 8.4 %collective-permute-start.1 = (f32[768,128]{1,0:T(8,128)S(1)}, f32[768,128]{1,0:T(8,128)S(1)}, u32[]{:S(2)}, u32[]{:S(2)}) collective-permute-start(f32[768,128]{1,0:T(8,128)S(1)} %get-tuple-element.29), channel_id=1, source_target_pairs={{0,32},{32,0},{1,33},{33,1},{2,34},{34,2},{3,35},{35,3},{4,36},{36... | collective-permute-start | bytes 1179656 | tf_op jit(solution)/shard_map/ppermute | solution.py:226
  17.8 4.4 %collective-permute-start.5 = (f32[768,128]{1,0:T(8,128)S(1)}, f32[768,128]{1,0:T(8,128)S(1)}, u32[]{:S(2)}, u32[]{:S(2)}) collective-permute-start(f32[768,128]{1,0:T(8,128)S(1)} %get-tuple-element.36), channel_id=1, source_target_pairs={{0,32},{32,0},{1,33},{33,1},{2,34},{34,2},{3,35},{35,3},{4,36},{36... | collective-permute-start | bytes 1179656 | tf_op jit(solution)/shard_map/ppermute | solution.py:226
  19.8 18.1 %collective-permute-start = (f32[768,128]{1,0:T(8,128)S(1)}, f32[768,128]{1,0:T(8,128)S(1)}, u32[]{:S(2)}, u32[]{:S(2)}) collective-permute-start(f32[768,128]{1,0:T(8,128)S(1)} %get-tuple-element.27), channel_id=1, source_target_pairs={{0,32},{32,0},{1,33},{33,1},{2,34},{34,2},{3,35},{35,3},{4,36},{36... | collective-permute-start | bytes 1179656 | tf_op jit(solution)/shard_map/ppermute | solution.py:226
  21.5 3.5 %collective-permute-start.13 = (f32[4,4,64,128]{3,2,1,0:T(8,128)S(1)}, f32[4,4,64,128]{3,2,1,0:T(8,128)S(1)}, u32[]{:S(2)}, u32[]{:S(2)}) collective-permute-start(f32[4,4,64,128]{3,2,1,0:T(8,128)S(1)} %get-tuple-element.41), channel_id=1, source_target_pairs={{0,32},{32,0},{1,33},{33,1},{2,34},{34,2},{3,35},{35,3},{4,36},{36... | collective-permute-start | bytes 1572872 | tf_op jit(solution)/shard_map/ppermute | solution.py:249
  22.1 7.7 %collective-permute-start.3 = (f32[384,128]{1,0:T(8,128)S(1)}, f32[384,128]{1,0:T(8,128)S(1)}, u32[]{:S(2)}, u32[]{:S(2)}) collective-permute-start(f32[384,128]{1,0:T(8,128)S(1)} %get-tuple-element.56), channel_id=1, source_target_pairs={{0,64},{64,128},{128,192},{192,0},{1,65},{65,129},{129,193},{193,1... | collective-permute-start | bytes 589832 | tf_op jit(solution)/shard_map/ppermute | solution.py:191
  22.2 7.6 %collective-permute-start.8 = (f32[384,128]{1,0:T(8,128)S(1)}, f32[384,128]{1,0:T(8,128)S(1)}, u32[]{:S(2)}, u32[]{:S(2)}) collective-permute-start(f32[384,128]{1,0:T(8,128)S(1)} %get-tuple-element.55), channel_id=1, source_target_pairs={{0,192},{64,0},{128,64},{192,128},{1,193},{65,1},{129,65},{193,129... | collective-permute-start | bytes 589832 | tf_op jit(solution)/shard_map/ppermute | solution.py:191
  24.9 39.5 %copy-start = (f32[8,32,128]{2,1,0:T(8,128)S(1)}, f32[8,32,128]{2,1,0:T(8,128)}, u32[]{:S(2)}) copy-start(f32[8,32,128]{2,1,0:T(8,128)} %hist_ref.1) | copy-start | bytes 393220
  24.9 39.5 %copy-start.1 = (f32[32,128]{1,0:T(8,128)S(1)}, f32[32,128]{1,0:T(8,128)}, u32[]{:S(2)}) copy-start(f32[32,128]{1,0:T(8,128)} %den_ref.1) | copy-start | bytes 49156
  24.9 13.0 %collective-permute-start.6 = (f32[384,128]{1,0:T(8,128)S(1)}, f32[384,128]{1,0:T(8,128)S(1)}, u32[]{:S(2)}, u32[]{:S(2)}) collective-permute-start(f32[384,128]{1,0:T(8,128)S(1)} %slice_add_fusion.3), channel_id=1, source_target_pairs={{0,192},{64,0},{128,64},{192,128},{1,193},{65,1},{129,65},{193,129... | collective-permute-start | bytes 589832 | tf_op jit(solution)/shard_map/ppermute | solution.py:191
  25.1 7.5 %collective-permute-start.14 = (f32[4,64,128]{2,1,0:T(8,128)S(1)}, f32[4,64,128]{2,1,0:T(8,128)S(1)}, u32[]{:S(2)}, u32[]{:S(2)}) collective-permute-start(f32[4,64,128]{2,1,0:T(8,128)S(1)} %get-tuple-element.50), channel_id=1, source_target_pairs={{0,16},{8,24},{16,0},{24,8},{1,17},{9,25},{17,1},{25,9},{2,18},{10... | collective-permute-start | bytes 393224 | tf_op jit(solution)/shard_map/ppermute | solution.py:191
  29.8 5.4 %collective-permute-start.15 = (f32[4,64,128]{2,1,0:T(8,128)S(1)}, f32[4,64,128]{2,1,0:T(8,128)S(1)}, u32[]{:S(2)}, u32[]{:S(2)}) collective-permute-start(f32[4,64,128]{2,1,0:T(8,128)S(1)} %get-tuple-element.52), channel_id=1, source_target_pairs={{0,8},{8,16},{16,24},{24,0},{1,9},{9,17},{17,25},{25,1},{2,10},{10... | collective-permute-start | bytes 393224 | tf_op jit(solution)/shard_map/ppermute | solution.py:191
  29.8 6.3 %collective-permute-start.16 = (f32[4,64,128]{2,1,0:T(8,128)S(1)}, f32[4,64,128]{2,1,0:T(8,128)S(1)}, u32[]{:S(2)}, u32[]{:S(2)}) collective-permute-start(f32[4,64,128]{2,1,0:T(8,128)S(1)} %get-tuple-element.51), channel_id=1, source_target_pairs={{0,24},{8,0},{16,8},{24,16},{1,25},{9,1},{17,9},{25,17},{2,26},{10... | collective-permute-start | bytes 393224 | tf_op jit(solution)/shard_map/ppermute | solution.py:191
  32.6 6.3 %collective-permute-start.7 = (f32[384,128]{1,0:T(8,128)S(1)}, f32[384,128]{1,0:T(8,128)S(1)}, u32[]{:S(2)}, u32[]{:S(2)}) collective-permute-start(f32[384,128]{1,0:T(8,128)S(1)} %slice_add_fusion.1), channel_id=1, source_target_pairs={{0,64},{64,128},{128,192},{192,0},{1,65},{65,129},{129,193},{193,1... | collective-permute-start | bytes 589832 | tf_op jit(solution)/shard_map/ppermute | solution.py:191
  35.2 8.1 %collective-permute-start.4 = (f32[384,128]{1,0:T(8,128)S(1)}, f32[384,128]{1,0:T(8,128)S(1)}, u32[]{:S(2)}, u32[]{:S(2)}) collective-permute-start(f32[384,128]{1,0:T(8,128)S(1)} %add_add_fusion.1), channel_id=1, source_target_pairs={{0,64},{64,128},{128,192},{192,0},{1,65},{65,129},{129,193},{193,1... | collective-permute-start | bytes 589832 | tf_op jit(solution)/shard_map/ppermute | solution.py:191
  36.2 7.2 %collective-permute-start.9 = (f32[384,128]{1,0:T(8,128)S(1)}, f32[384,128]{1,0:T(8,128)S(1)}, u32[]{:S(2)}, u32[]{:S(2)}) collective-permute-start(f32[384,128]{1,0:T(8,128)S(1)} %add_add_fusion), channel_id=1, source_target_pairs={{0,192},{64,0},{128,64},{192,128},{1,193},{65,1},{129,65},{193,129... | collective-permute-start | bytes 589832 | tf_op jit(solution)/shard_map/ppermute | solution.py:191
  43.4 12.1 %collective-permute-start.10 = (f32[192,128]{1,0:T(8,128)S(1)}, f32[192,128]{1,0:T(8,128)S(1)}, u32[]{:S(2)}, u32[]{:S(2)}) collective-permute-start(f32[192,128]{1,0:T(8,128)S(1)} %get-tuple-element.58), channel_id=1, source_target_pairs={{0,16},{8,24},{16,0},{24,8},{1,17},{9,25},{17,1},{25,9},{2,18},{10... | collective-permute-start | bytes 294920 | tf_op jit(solution)/shard_map/ppermute | solution.py:191
  45.3 10.3 %collective-permute-start.11 = (f32[192,128]{1,0:T(8,128)S(1)}, f32[192,128]{1,0:T(8,128)S(1)}, u32[]{:S(2)}, u32[]{:S(2)}) collective-permute-start(f32[192,128]{1,0:T(8,128)S(1)} %get-tuple-element.59), channel_id=1, source_target_pairs={{0,8},{8,16},{16,24},{24,0},{1,9},{9,17},{17,25},{25,1},{2,10},{10... | collective-permute-start | bytes 294920 | tf_op jit(solution)/shard_map/ppermute | solution.py:191
  45.4 10.2 %collective-permute-start.12 = (f32[192,128]{1,0:T(8,128)S(1)}, f32[192,128]{1,0:T(8,128)S(1)}, u32[]{:S(2)}, u32[]{:S(2)}) collective-permute-start(f32[192,128]{1,0:T(8,128)S(1)} %get-tuple-element.57), channel_id=1, source_target_pairs={{0,24},{8,0},{16,8},{24,16},{1,25},{9,1},{17,9},{25,17},{2,26},{10... | collective-permute-start | bytes 294920 | tf_op jit(solution)/shard_map/ppermute | solution.py:191
  48.0 4.5 %collective-permute-start.17 = (f32[64,128]{1,0:T(8,128)S(1)}, f32[64,128]{1,0:T(8,128)S(1)}, u32[]{:S(2)}, u32[]{:S(2)}) collective-permute-start(f32[64,128]{1,0:T(8,128)S(1)} %get-tuple-element.63), channel_id=1, source_target_pairs={{0,128},{64,192},{128,0},{192,64},{1,129},{65,193},{129,1},{193,65... | collective-permute-start | bytes 98312 | tf_op jit(solution)/shard_map/ppermute | solution.py:191
  48.1 5.3 %collective-permute-start.18 = (f32[64,128]{1,0:T(8,128)S(1)}, f32[64,128]{1,0:T(8,128)S(1)}, u32[]{:S(2)}, u32[]{:S(2)}) collective-permute-start(f32[64,128]{1,0:T(8,128)S(1)} %get-tuple-element.62), channel_id=1, source_target_pairs={{0,64},{64,128},{128,192},{192,0},{1,65},{65,129},{129,193},{193,1... | collective-permute-start | bytes 98312 | tf_op jit(solution)/shard_map/ppermute | solution.py:191
  52.5 3.1 %collective-permute-start.19 = (f32[64,128]{1,0:T(8,128)S(1)}, f32[64,128]{1,0:T(8,128)S(1)}, u32[]{:S(2)}, u32[]{:S(2)}) collective-permute-start(f32[64,128]{1,0:T(8,128)S(1)} %get-tuple-element.61), channel_id=1, source_target_pairs={{0,192},{64,0},{128,64},{192,128},{1,193},{65,1},{129,65},{193,129... | collective-permute-start | bytes 98312 | tf_op jit(solution)/shard_map/ppermute | solution.py:191
  56.2 16.0 %all-to-all-start = ((f32[8,32,128]{2,1,0:T(8,128)}), f32[8,32,128]{2,1,0:T(8,128)S(1)}, u32[]{:S(2)}, u32[]{:S(2)}) async-start(f32[8,32,128]{2,1,0:T(8,128)} %join.1), calls=%async_computation | async-start | bytes 262144 | tf_op jit(solution)/shard_map/all_to_all | solution.py:267

commit v5 on v3

--- a/solution.py
+++ b/solution.py
@@ -134,7 +134,8 @@
     message = early_ref[...]
     for l in range(HIST):
         message = gram_entry(errors, HIST - 1, l, lane, message)
-    message_ref[...] = message
+    for s in range(32):
+        message_ref[s * 8:(s + 1) * 8, :] = message
 
 
 def tail_kernel(grams_ref, update_ref, following_ref, out_ref, coef_ref):
@@ -249,13 +250,11 @@
     parts = lax.all_to_all(rows, "z", 0, 0, tiled=True)
     update, message = pl.pallas_call(
         gram_kernel,
-        out_shape=(block, jax.ShapeDtypeStruct((8, LANES), jnp.float32)),
+        out_shape=(block, jax.ShapeDtypeStruct((256, LANES), jnp.float32)),
         compiler_params=SMALL,
         name="gram",
     )(parts, divisors, errors, following, early)
-    message = message + lax.ppermute(message, "core", [(0, 1), (1, 0)])
-    message = jnp.broadcast_to(message, (16, 8, LANES)).reshape(16 * 8, LANES)
-    grams = lax.all_to_all(message, ("x", "y", "z"), 0, 0, tiled=True)
+    grams = lax.all_to_all(message, ("x", "core", "y", "z"), 0, 0, tiled=True)
     extrapolated, coefficients = pl.pallas_call(
         tail_kernel,
         out_shape=(block, jax.ShapeDtypeStruct((1, HIST), jnp.float32)),

time: 98.8 us -> 99 us (level)
  blocking collectives: 17.1 us -> 23 us
  starting transfers between devices: 38 us -> 33.1 us
    all_to_all x1, blocking collectives: 17.1 us -> 23 us  [step(): grams = lax.all_to_all(message, ('x', 'core', 'y', 'z'), 0, 0, tiled=True)]
    ppermute x1 -> x0, starting transfers between devices: 4.85 us -> none  [step(): message = message + lax.ppermute(message, 'core', [(0, 1), (1, 0)])]
  transfers between devices with their start and end apart: 19 -> 18, of which waited for: 7 -> 6; matrix products, arithmetic and copies ran while one was open for 0% -> 0% of each run, Pallas kernels for 5% -> 5%
where the time goes in v5:
time: 99 us; the launch traced here: 98.8 us
  starting transfers between devices  33.1 us (33%)
  waiting for transfers between devices  23 us (23%)
  blocking collectives  23 us (23%)
  matrix products  9.45 us (10%)
  Pallas kernels  8.97 us (9%)
    all_to_all x1, blocking collectives, step(): grams = lax.all_to_all(message, ('x', 'core', 'y', 'z'), 0, 0, tiled=True)  23 us
    ppermute x12, starting transfers between devices, shift(): lax.ppermute(value, axis, [(i, (i + distance) % 4) for i in range(4)])  19.6 us
    ppermute x12, waiting for transfers between devices, shift(): lax.ppermute(value, axis, [(i, (i + distance) % 4) for i in range(4)])  15.2 us
    dot_general x2, matrix products, product(): lax.dot_general(a, b, (((0,), (0,)), ((), ())), precision=lax.Precision.H...  9.45 us
    all_to_all x1, starting transfers between devices, step(): parts = lax.all_to_all(rows, 'z', 0, 0, tiled=True)  8.19 us
    all_to_all x1, waiting for transfers between devices, step(): parts = lax.all_to_all(rows, 'z', 0, 0, tiled=True)  7.74 us
    pallas_call x5, Pallas kernels, mirrored(): pl.pallas_call(kernel, out_shape=(out, out), scratch_shapes=[pltpu.VMEM(s...  6.44 us
    ppermute x5, starting transfers between devices, step(): came = lax.ppermute(sent, 'core', [(0, 1), (1, 0)])  5.37 us
  transfers between devices with their start and end apart: 18, of which 6 were waited for; matrix products, arithmetic and copies ran while one was open for 0% of the time, Pallas kernels for 5%

profile of v5, /device:TPU:1, one launch (start us, length us, event | category | flops | bytes accessed | tf_op | source)
XLA Modules:
  0.0 98.8 jit_solution(13341940463980435795)
XLA Ops:
  0.6 0.6 hot.1.refs_1_.hot_ref
  1.2 0.0 copy-start.2
  1.3 0.0 copy-start.3
  1.3 5.9 %fusion.2 = f32[1024,1024]{1,0:T(8,128)S(1)} fusion(f32[1024,1024]{1,0:T(8,128)} %param.5, f32[1024,1024]{1,0:T(8,128)} %param.4), kind=kOutput, calls=%fused_computation.3 | convolution fusion | flops 3221225472 | bytes 8388608 | tf_op jit(solution)/shard_map/dot_general | solution.py:195
  7.2 0.0 copy-done.2
  7.2 0.0 copy-done.3
  7.2 3.6 %convolution_add_fusion.refs_0_.p_ref = f32[1024,1024]{1,0:T(8,128)S(1)} fusion(f32[1024,1024]{1,0:T(8,128)S(1)} %fusion.2, f32[1024,1024]{1,0:T(8,128)S(1)} %copy-done.2, f32[1024,1024]{1,0:T(8,128)S(1)} %copy-done.3), kind=kOutput, calls=%fused_computation | convolution fusion | flops 3222274048 | bytes 12582912 | tf_op jit(solution)/shard_map/dot_general | solution.py:195
  10.7 1.6 %shard_map.63 = (f32[4,4,64,128]{3,2,1,0:T(8,128)S(1)}, f32[4,4,64,128]{3,2,1,0:T(8,128)S(1)}) custom-call(f32[1024,1024]{1,0:T(8,128)S(1)} %convolution_add_fusion.refs_0_.p_ref, bf16[1024,1024]{1,0:T(8,128)(2,1)S(1)} %hot.1.refs_1_.hot_ref), custom_call_target="tpu_custom_call" | custom-call | flops 1073741824 | bytes 5242880 | tf_op jit(solution)/shard_map/pallas_call | solution.py:84
  12.3 3.3 %collective-permute-start.10 = (f32[4,4,64,128]{3,2,1,0:T(8,128)S(1)}, f32[4,4,64,128]{3,2,1,0:T(8,128)S(1)}, u32[]{:S(2)}, u32[]{:S(2)}) collective-permute-start(f32[4,4,64,128]{3,2,1,0:T(8,128)S(1)} %get-tuple-element.29), channel_id=1, source_target_pairs={{0,32},{32,0},{1,33},{33,1},{2,34},{34,2},{3,35},{35,3},{4,36},{36... | collective-permute-start | bytes 1572872 | tf_op jit(solution)/shard_map/ppermute | solution.py:233
  15.6 1.2 %shard_map.60 = (f32[768,128]{1,0:T(8,128)S(1)}, f32[768,128]{1,0:T(8,128)S(1)}) custom-call(f32[1024,1024]{1,0:T(8,128)S(1)} %convolution_add_fusion.refs_0_.p_ref, bf16[1024,1024]{1,0:T(8,128)(2,1)S(1)} %hot.1.refs_1_.hot_ref), custom_call_target="tpu_custom_call" | custom-call | flops 1073741824 | bytes 5242880 | tf_op jit(solution)/shard_map/pallas_call | solution.py:84
  16.9 0.3 collective-permute-start.1
  17.1 1.2 %shard_map.61 = (f32[768,128]{1,0:T(8,128)S(1)}, f32[768,128]{1,0:T(8,128)S(1)}) custom-call(f32[1024,1024]{1,0:T(8,128)S(1)} %convolution_add_fusion.refs_0_.p_ref, bf16[1024,1024]{1,0:T(8,128)(2,1)S(1)} %hot.1.refs_1_.hot_ref), custom_call_target="tpu_custom_call" | custom-call | flops 1073741824 | bytes 5242880 | tf_op jit(solution)/shard_map/pallas_call | solution.py:84
  18.4 0.6 collective-permute-start.3
  18.9 1.2 %shard_map.62 = (f32[768,128]{1,0:T(8,128)S(1)}, f32[768,128]{1,0:T(8,128)S(1)}) custom-call(f32[1024,1024]{1,0:T(8,128)S(1)} %convolution_add_fusion.refs_0_.p_ref, bf16[1024,1024]{1,0:T(8,128)(2,1)S(1)} %hot.1.refs_1_.hot_ref), custom_call_target="tpu_custom_call" | custom-call | flops 1073741824 | bytes 5242880 | tf_op jit(solution)/shard_map/pallas_call | solution.py:84
  20.2 0.1 collective-permute-start.5
  20.3 0.0 collective-permute-done.10
  20.3 1.3 %collective-permute-start.11 = (f32[4,64,128]{2,1,0:T(8,128)S(1)}, f32[4,64,128]{2,1,0:T(8,128)S(1)}, u32[]{:S(2)}, u32[]{:S(2)}) collective-permute-start(f32[4,64,128]{2,1,0:T(8,128)S(1)} %get-tuple-element.38), channel_id=1, source_target_pairs={{0,16},{8,24},{16,0},{24,8},{1,17},{9,25},{17,1},{25,9},{2,18},{10... | collective-permute-start | bytes 393224 | tf_op jit(solution)/shard_map/ppermute | solution.py:191
  21.6 0.4 collective-permute-start.12
  22.0 1.2 %shard_map.59 = (f32[768,128]{1,0:T(8,128)S(1)}, f32[768,128]{1,0:T(8,128)S(1)}) custom-call(f32[1024,1024]{1,0:T(8,128)S(1)} %convolution_add_fusion.refs_0_.p_ref, bf16[1024,1024]{1,0:T(8,128)(2,1)S(1)} %hot.1.refs_1_.hot_ref), custom_call_target="tpu_custom_call" | custom-call | flops 1073741824 | bytes 5242880 | tf_op jit(solution)/shard_map/pallas_call | solution.py:84
  23.2 0.0 collective-permute-done.1
  23.2 1.1 %collective-permute-start = (f32[768,128]{1,0:T(8,128)S(1)}, f32[768,128]{1,0:T(8,128)S(1)}, u32[]{:S(2)}, u32[]{:S(2)}) collective-permute-start(f32[768,128]{1,0:T(8,128)S(1)} %get-tuple-element.21), channel_id=1, source_target_pairs={{0,32},{32,0},{1,33},{33,1},{2,34},{34,2},{3,35},{35,3},{4,36},{36... | collective-permute-start | bytes 1179656 | tf_op jit(solution)/shard_map/ppermute | solution.py:226
  24.4 0.0 copy-start
  24.4 0.0 copy-start.1
  24.4 0.0 collective-permute-done.3
  24.4 2.9 %collective-permute-start.2 = (f32[768,128]{1,0:T(8,128)S(1)}, f32[768,128]{1,0:T(8,128)S(1)}, u32[]{:S(2)}, u32[]{:S(2)}) collective-permute-start(f32[768,128]{1,0:T(8,128)S(1)} %add.59), channel_id=1, source_target_pairs={{0,128},{64,192},{128,0},{192,64},{1,129},{65,193},{129,1},{193,65... | collective-permute-start | bytes 1179656 | tf_op jit(solution)/shard_map/ppermute | solution.py:191
  27.3 0.0 collective-permute-done.5
  27.3 0.4 collective-permute-start.4
  27.8 0.0 collective-permute-done.11
  27.8 2.4 %collective-permute-start.6 = (f32[768,128]{1,0:T(8,128)S(1)}, f32[768,128]{1,0:T(8,128)S(1)}, u32[]{:S(2)}, u32[]{:S(2)}) collective-permute-start(f32[768,128]{1,0:T(8,128)S(1)} %add.63), channel_id=1, source_target_pairs={{0,192},{64,0},{128,64},{192,128},{1,193},{65,1},{129,65},{193,129... | collective-permute-start | bytes 1179656 | tf_op jit(solution)/shard_map/ppermute | solution.py:191
  30.2 0.0 collective-permute-done.12
  30.2 2.2 %collective-permute-start.13 = (f32[4,64,128]{2,1,0:T(8,128)S(1)}, f32[4,64,128]{2,1,0:T(8,128)S(1)}, u32[]{:S(2)}, u32[]{:S(2)}) collective-permute-start(f32[4,64,128]{2,1,0:T(8,128)S(1)} %get-tuple-element.39), channel_id=1, source_target_pairs={{0,24},{8,0},{16,8},{24,16},{1,25},{9,1},{17,9},{25,17},{2,26},{10... | collective-permute-start | bytes 393224 | tf_op jit(solution)/shard_map/ppermute | solution.py:191
  32.5 1.9 %collective-permute-done.13 = f32[4,64,128]{2,1,0:T(8,128)S(1)} collective-permute-done((f32[4,64,128]{2,1,0:T(8,128)S(1)}, f32[4,64,128]{2,1,0:T(8,128)S(1)}, u32[]{:S(2)}, u32[]{:S(2)}) %collective-permute-start.13) | collective-permute-done | bytes 131104 | tf_op jit(solution)/shard_map/ppermute | solution.py:191
  34.5 0.0 collective-permute-done
  34.5 2.2 %collective-permute-done.2 = f32[768,128]{1,0:T(8,128)S(1)} collective-permute-done((f32[768,128]{1,0:T(8,128)S(1)}, f32[768,128]{1,0:T(8,128)S(1)}, u32[]{:S(2)}, u32[]{:S(2)}) %collective-permute-start.2) | collective-permute-done | bytes 393248 | tf_op jit(solution)/shard_map/ppermute | solution.py:191
  36.7 8.8 %collective-permute-done.4 = f32[768,128]{1,0:T(8,128)S(1)} collective-permute-done((f32[768,128]{1,0:T(8,128)S(1)}, f32[768,128]{1,0:T(8,128)S(1)}, u32[]{:S(2)}, u32[]{:S(2)}) %collective-permute-start.4) | collective-permute-done | bytes 393248 | tf_op jit(solution)/shard_map/ppermute | solution.py:191
  45.5 0.0 collective-permute-done.6
  45.5 0.1 add_add_fusion
  45.6 1.7 %collective-permute-start.7 = (f32[192,128]{1,0:T(8,128)S(1)}, f32[192,128]{1,0:T(8,128)S(1)}, u32[]{:S(2)}, u32[]{:S(2)}) collective-permute-start(f32[192,128]{1,0:T(8,128)S(1)} %get-tuple-element.43), channel_id=1, source_target_pairs={{0,16},{8,24},{16,0},{24,8},{1,17},{9,25},{17,1},{25,9},{2,18},{10... | collective-permute-start | bytes 294920 | tf_op jit(solution)/shard_map/ppermute | solution.py:191
  47.3 1.3 %collective-permute-start.8 = (f32[192,128]{1,0:T(8,128)S(1)}, f32[192,128]{1,0:T(8,128)S(1)}, u32[]{:S(2)}, u32[]{:S(2)}) collective-permute-start(f32[192,128]{1,0:T(8,128)S(1)} %get-tuple-element.42), channel_id=1, source_target_pairs={{0,8},{8,16},{16,24},{24,0},{1,9},{9,17},{17,25},{25,1},{2,10},{10... | collective-permute-start | bytes 294920 | tf_op jit(solution)/shard_map/ppermute | solution.py:191
  48.6 1.4 %collective-permute-start.9 = (f32[192,128]{1,0:T(8,128)S(1)}, f32[192,128]{1,0:T(8,128)S(1)}, u32[]{:S(2)}, u32[]{:S(2)}) collective-permute-start(f32[192,128]{1,0:T(8,128)S(1)} %get-tuple-element.41), channel_id=1, source_target_pairs={{0,24},{8,0},{16,8},{24,16},{1,25},{9,1},{17,9},{25,17},{2,26},{10... | collective-permute-start | bytes 294920 | tf_op jit(solution)/shard_map/ppermute | solution.py:191
  50.0 1.7 %collective-permute-start.14 = (f32[64,128]{1,0:T(8,128)S(1)}, f32[64,128]{1,0:T(8,128)S(1)}, u32[]{:S(2)}, u32[]{:S(2)}) collective-permute-start(f32[64,128]{1,0:T(8,128)S(1)} %get-tuple-element.47), channel_id=1, source_target_pairs={{0,128},{64,192},{128,0},{192,64},{1,129},{65,193},{129,1},{193,65... | collective-permute-start | bytes 98312 | tf_op jit(solution)/shard_map/ppermute | solution.py:191
  51.7 1.4 %collective-permute-start.15 = (f32[64,128]{1,0:T(8,128)S(1)}, f32[64,128]{1,0:T(8,128)S(1)}, u32[]{:S(2)}, u32[]{:S(2)}) collective-permute-start(f32[64,128]{1,0:T(8,128)S(1)} %get-tuple-element.46), channel_id=1, source_target_pairs={{0,64},{64,128},{128,192},{192,0},{1,65},{65,129},{129,193},{193,1... | collective-permute-start | bytes 98312 | tf_op jit(solution)/shard_map/ppermute | solution.py:191
  53.1 1.2 %collective-permute-done.14.refs_5_ = f32[64,128]{1,0:T(8,128)S(1)} collective-permute-done((f32[64,128]{1,0:T(8,128)S(1)}, f32[64,128]{1,0:T(8,128)S(1)}, u32[]{:S(2)}, u32[]{:S(2)}) %collective-permute-start.14) | collective-permute-done | bytes 32800 | tf_op jit(solution)/shard_map/ppermute | solution.py:191
  54.3 2.5 %collective-permute-start.16 = (f32[64,128]{1,0:T(8,128)S(1)}, f32[64,128]{1,0:T(8,128)S(1)}, u32[]{:S(2)}, u32[]{:S(2)}) collective-permute-start(f32[64,128]{1,0:T(8,128)S(1)} %get-tuple-element.45), channel_id=1, source_target_pairs={{0,192},{64,0},{128,64},{192,128},{1,193},{65,1},{129,65},{193,129... | collective-permute-start | bytes 98312 | tf_op jit(solution)/shard_map/ppermute | solution.py:191
  56.8 0.0 collective-permute-done.15.refs_6_
  56.8 1.0 %collective-permute-done.16.refs_7_ = f32[64,128]{1,0:T(8,128)S(1)} collective-permute-done((f32[64,128]{1,0:T(8,128)S(1)}, f32[64,128]{1,0:T(8,128)S(1)}, u32[]{:S(2)}, u32[]{:S(2)}) %collective-permute-start.16) | collective-permute-done | bytes 32800 | tf_op jit(solution)/shard_map/ppermute | solution.py:191
  57.8 0.0 collective-permute-done.7.refs_1_
  57.8 0.0 collective-permute-done.8.refs_2_
  57.8 0.0 collective-permute-done.9.refs_3_
  57.8 0.7 join.1
  58.5 8.2 %all-to-all-start = ((f32[8,32,128]{2,1,0:T(8,128)}), f32[8,32,128]{2,1,0:T(8,128)S(1)}, u32[]{:S(2)}, u32[]{:S(2)}) async-start(f32[8,32,128]{2,1,0:T(8,128)} %join.1), calls=%async_computation | async-start | bytes 262144 | tf_op jit(solution)/shard_map/all_to_all | solution.py:250
  66.7 0.0 copy-done
  66.7 0.0 copy-done.1
  66.7 0.2 prepare.1
  66.9 7.7 %all-to-all-done.parts_ref = f32[8,32,128]{2,1,0:T(8,128)S(1)} async-done(((f32[8,32,128]{2,1,0:T(8,128)}), f32[8,32,128]{2,1,0:T(8,128)S(1)}, u32[]{:S(2)}, u32[]{:S(2)}) %all-to-all-start) | async-done | bytes 131104 | tf_op jit(solution)/shard_map/all_to_all | solution.py:250
  74.6 0.1 gram.1
  74.8 23.0 %all_to_all.16 = f32[256,1,128]{2,1,0:T(1,128)S(1)} all-to-all(f32[256,1,128]{2,1,0:T(1,128)S(1)} %bitcast.28), channel_id=1, replica_groups=mesh['x'=4,'core'=2,'y'=4,'z'=8] {'x','core','y','z'}, dimensions={0} | all-to-all | bytes 262144 | tf_op jit(solution)/shard_map/all_to_all | solution.py:257
  97.8 0.9 tail.1
  (7 shorter events, 0.2 us)
Async XLA Ops:
  1.2 5.9 %copy-start.2 = (f32[1024,1024]{1,0:T(8,128)S(1)}, f32[1024,1024]{1,0:T(8,128)}, u32[]{:S(2)}) copy-start(f32[1024,1024]{1,0:T(8,128)} %param.5) | copy-start | bytes 12582916
  1.3 5.9 %copy-start.3 = (f32[1024,1024]{1,0:T(8,128)S(1)}, f32[1024,1024]{1,0:T(8,128)}, u32[]{:S(2)}) copy-start(f32[1024,1024]{1,0:T(8,128)} %param.4) | copy-start | bytes 12582916
  12.3 7.9 %collective-permute-start.10 = (f32[4,4,64,128]{3,2,1,0:T(8,128)S(1)}, f32[4,4,64,128]{3,2,1,0:T(8,128)S(1)}, u32[]{:S(2)}, u32[]{:S(2)}) collective-permute-start(f32[4,4,64,128]{3,2,1,0:T(8,128)S(1)} %get-tuple-element.29), channel_id=1, source_target_pairs={{0,32},{32,0},{1,33},{33,1},{2,34},{34,2},{3,35},{35,3},{4,36},{36... | collective-permute-start | bytes 1572872 | tf_op jit(solution)/shard_map/ppermute | solution.py:233
  16.9 6.4 %collective-permute-start.1 = (f32[768,128]{1,0:T(8,128)S(1)}, f32[768,128]{1,0:T(8,128)S(1)}, u32[]{:S(2)}, u32[]{:S(2)}) collective-permute-start(f32[768,128]{1,0:T(8,128)S(1)} %get-tuple-element.23), channel_id=1, source_target_pairs={{0,32},{32,0},{1,33},{33,1},{2,34},{34,2},{3,35},{35,3},{4,36},{36... | collective-permute-start | bytes 1179656 | tf_op jit(solution)/shard_map/ppermute | solution.py:226
  18.4 6.0 %collective-permute-start.3 = (f32[768,128]{1,0:T(8,128)S(1)}, f32[768,128]{1,0:T(8,128)S(1)}, u32[]{:S(2)}, u32[]{:S(2)}) collective-permute-start(f32[768,128]{1,0:T(8,128)S(1)} %get-tuple-element.25), channel_id=1, source_target_pairs={{0,32},{32,0},{1,33},{33,1},{2,34},{34,2},{3,35},{35,3},{4,36},{36... | collective-permute-start | bytes 1179656 | tf_op jit(solution)/shard_map/ppermute | solution.py:226
  20.2 7.2 %collective-permute-start.5 = (f32[768,128]{1,0:T(8,128)S(1)}, f32[768,128]{1,0:T(8,128)S(1)}, u32[]{:S(2)}, u32[]{:S(2)}) collective-permute-start(f32[768,128]{1,0:T(8,128)S(1)} %get-tuple-element.27), channel_id=1, source_target_pairs={{0,32},{32,0},{1,33},{33,1},{2,34},{34,2},{3,35},{35,3},{4,36},{36... | collective-permute-start | bytes 1179656 | tf_op jit(solution)/shard_map/ppermute | solution.py:226
  20.3 7.5 %collective-permute-start.11 = (f32[4,64,128]{2,1,0:T(8,128)S(1)}, f32[4,64,128]{2,1,0:T(8,128)S(1)}, u32[]{:S(2)}, u32[]{:S(2)}) collective-permute-start(f32[4,64,128]{2,1,0:T(8,128)S(1)} %get-tuple-element.38), channel_id=1, source_target_pairs={{0,16},{8,24},{16,0},{24,8},{1,17},{9,25},{17,1},{25,9},{2,18},{10... | collective-permute-start | bytes 393224 | tf_op jit(solution)/shard_map/ppermute | solution.py:191
  21.6 8.6 %collective-permute-start.12 = (f32[4,64,128]{2,1,0:T(8,128)S(1)}, f32[4,64,128]{2,1,0:T(8,128)S(1)}, u32[]{:S(2)}, u32[]{:S(2)}) collective-permute-start(f32[4,64,128]{2,1,0:T(8,128)S(1)} %get-tuple-element.40), channel_id=1, source_target_pairs={{0,8},{8,16},{16,24},{24,0},{1,9},{9,17},{17,25},{25,1},{2,10},{10... | collective-permute-start | bytes 393224 | tf_op jit(solution)/shard_map/ppermute | solution.py:191
  23.2 11.2 %collective-permute-start = (f32[768,128]{1,0:T(8,128)S(1)}, f32[768,128]{1,0:T(8,128)S(1)}, u32[]{:S(2)}, u32[]{:S(2)}) collective-permute-start(f32[768,128]{1,0:T(8,128)S(1)} %get-tuple-element.21), channel_id=1, source_target_pairs={{0,32},{32,0},{1,33},{33,1},{2,34},{34,2},{3,35},{35,3},{4,36},{36... | collective-permute-start | bytes 1179656 | tf_op jit(solution)/shard_map/ppermute | solution.py:226
  24.4 42.3 %copy-start = (f32[8,32,128]{2,1,0:T(8,128)S(1)}, f32[8,32,128]{2,1,0:T(8,128)}, u32[]{:S(2)}) copy-start(f32[8,32,128]{2,1,0:T(8,128)} %hist_ref.1) | copy-start | bytes 393220
  24.4 42.3 %copy-start.1 = (f32[32,128]{1,0:T(8,128)S(1)}, f32[32,128]{1,0:T(8,128)}, u32[]{:S(2)}) copy-start(f32[32,128]{1,0:T(8,128)} %den_ref.1) | copy-start | bytes 49156
  24.4 12.3 %collective-permute-start.2 = (f32[768,128]{1,0:T(8,128)S(1)}, f32[768,128]{1,0:T(8,128)S(1)}, u32[]{:S(2)}, u32[]{:S(2)}) collective-permute-start(f32[768,128]{1,0:T(8,128)S(1)} %add.59), channel_id=1, source_target_pairs={{0,128},{64,192},{128,0},{192,64},{1,129},{65,193},{129,1},{193,65... | collective-permute-start | bytes 1179656 | tf_op jit(solution)/shard_map/ppermute | solution.py:191
  27.3 18.2 %collective-permute-start.4 = (f32[768,128]{1,0:T(8,128)S(1)}, f32[768,128]{1,0:T(8,128)S(1)}, u32[]{:S(2)}, u32[]{:S(2)}) collective-permute-start(f32[768,128]{1,0:T(8,128)S(1)} %add.61), channel_id=1, source_target_pairs={{0,64},{64,128},{128,192},{192,0},{1,65},{65,129},{129,193},{193,1... | collective-permute-start | bytes 1179656 | tf_op jit(solution)/shard_map/ppermute | solution.py:191
  27.8 17.7 %collective-permute-start.6 = (f32[768,128]{1,0:T(8,128)S(1)}, f32[768,128]{1,0:T(8,128)S(1)}, u32[]{:S(2)}, u32[]{:S(2)}) collective-permute-start(f32[768,128]{1,0:T(8,128)S(1)} %add.63), channel_id=1, source_target_pairs={{0,192},{64,0},{128,64},{192,128},{1,193},{65,1},{129,65},{193,129... | collective-permute-start | bytes 1179656 | tf_op jit(solution)/shard_map/ppermute | solution.py:191
  30.2 4.2 %collective-permute-start.13 = (f32[4,64,128]{2,1,0:T(8,128)S(1)}, f32[4,64,128]{2,1,0:T(8,128)S(1)}, u32[]{:S(2)}, u32[]{:S(2)}) collective-permute-start(f32[4,64,128]{2,1,0:T(8,128)S(1)} %get-tuple-element.39), channel_id=1, source_target_pairs={{0,24},{8,0},{16,8},{24,16},{1,25},{9,1},{17,9},{25,17},{2,26},{10... | collective-permute-start | bytes 393224 | tf_op jit(solution)/shard_map/ppermute | solution.py:191
  45.6 12.2 %collective-permute-start.7 = (f32[192,128]{1,0:T(8,128)S(1)}, f32[192,128]{1,0:T(8,128)S(1)}, u32[]{:S(2)}, u32[]{:S(2)}) collective-permute-start(f32[192,128]{1,0:T(8,128)S(1)} %get-tuple-element.43), channel_id=1, source_target_pairs={{0,16},{8,24},{16,0},{24,8},{1,17},{9,25},{17,1},{25,9},{2,18},{10... | collective-permute-start | bytes 294920 | tf_op jit(solution)/shard_map/ppermute | solution.py:191
  47.3 10.5 %collective-permute-start.8 = (f32[192,128]{1,0:T(8,128)S(1)}, f32[192,128]{1,0:T(8,128)S(1)}, u32[]{:S(2)}, u32[]{:S(2)}) collective-permute-start(f32[192,128]{1,0:T(8,128)S(1)} %get-tuple-element.42), channel_id=1, source_target_pairs={{0,8},{8,16},{16,24},{24,0},{1,9},{9,17},{17,25},{25,1},{2,10},{10... | collective-permute-start | bytes 294920 | tf_op jit(solution)/shard_map/ppermute | solution.py:191
  48.6 9.2 %collective-permute-start.9 = (f32[192,128]{1,0:T(8,128)S(1)}, f32[192,128]{1,0:T(8,128)S(1)}, u32[]{:S(2)}, u32[]{:S(2)}) collective-permute-start(f32[192,128]{1,0:T(8,128)S(1)} %get-tuple-element.41), channel_id=1, source_target_pairs={{0,24},{8,0},{16,8},{24,16},{1,25},{9,1},{17,9},{25,17},{2,26},{10... | collective-permute-start | bytes 294920 | tf_op jit(solution)/shard_map/ppermute | solution.py:191
  50.0 4.4 %collective-permute-start.14 = (f32[64,128]{1,0:T(8,128)S(1)}, f32[64,128]{1,0:T(8,128)S(1)}, u32[]{:S(2)}, u32[]{:S(2)}) collective-permute-start(f32[64,128]{1,0:T(8,128)S(1)} %get-tuple-element.47), channel_id=1, source_target_pairs={{0,128},{64,192},{128,0},{192,64},{1,129},{65,193},{129,1},{193,65... | collective-permute-start | bytes 98312 | tf_op jit(solution)/shard_map/ppermute | solution.py:191
  51.7 5.1 %collective-permute-start.15 = (f32[64,128]{1,0:T(8,128)S(1)}, f32[64,128]{1,0:T(8,128)S(1)}, u32[]{:S(2)}, u32[]{:S(2)}) collective-permute-start(f32[64,128]{1,0:T(8,128)S(1)} %get-tuple-element.46), channel_id=1, source_target_pairs={{0,64},{64,128},{128,192},{192,0},{1,65},{65,129},{129,193},{193,1... | collective-permute-start | bytes 98312 | tf_op jit(solution)/shard_map/ppermute | solution.py:191
  54.3 3.5 %collective-permute-start.16 = (f32[64,128]{1,0:T(8,128)S(1)}, f32[64,128]{1,0:T(8,128)S(1)}, u32[]{:S(2)}, u32[]{:S(2)}) collective-permute-start(f32[64,128]{1,0:T(8,128)S(1)} %get-tuple-element.45), channel_id=1, source_target_pairs={{0,192},{64,0},{128,64},{192,128},{1,193},{65,1},{129,65},{193,129... | collective-permute-start | bytes 98312 | tf_op jit(solution)/shard_map/ppermute | solution.py:191
  58.5 16.1 %all-to-all-start = ((f32[8,32,128]{2,1,0:T(8,128)}), f32[8,32,128]{2,1,0:T(8,128)S(1)}, u32[]{:S(2)}, u32[]{:S(2)}) async-start(f32[8,32,128]{2,1,0:T(8,128)} %join.1), calls=%async_computation | async-start | bytes 262144 | tf_op jit(solution)/shard_map/all_to_all | solution.py:250
